TPU v7x, 256 devices: a whole 4x4x8 slice. The times are simulated.
256 devices in a mesh: row: 32 (over z_hi, x, core), col: 8 (over z_lo, y).
Axes of the slice: x: 4, y: 4, z: 8 (z_hi: 4, z_lo: 2; z = z_hi * 2 + z_lo), core: 2. Of those that a mesh axis runs over, the one named last changes fastest.
Arguments:
- left_act: bfloat16 [1024, 4096], P('row', 'col'), may hold values from -18 to 18
- right_act: bfloat16 [1024, 4096], P('col', 'row'), may hold values from -18 to 18
- out_weight: bfloat16 [1024, 128], replicated, may hold values from -0.1875 to 0.1875
- out_bias: float32 [128], replicated, may hold values from -1 to 1
- pair_grad: bfloat16 [1024, 1024, 128], P('row', 'col'), may hold values from -13 to 13
Outputs:
- pair_out: bfloat16 [1024, 1024, 128], P('row', 'col')
- left_grad: float32 [1024, 4096], P('row', 'col')
- right_grad: float32 [1024, 4096], P('col', 'row')
- weight_grad: float32 [1024, 128], replicated
- bias_grad: float32 [128], replicated
All inputs are finite; a program needn't handle non-finite values.
Results may differ from a plain program's by a relative error of at most 0.005.
Values may be sent and summed in bfloat16 or wider, within the bound.
No kernel may reach another device: no remote copies, remote signals or barrier semaphores. Data moves between devices by JAX's collectives and lax.ppermute only.
A program may use at most 128 MiB of HBM per device.

v0:
```python
import jax
import jax.numpy as jnp
from jax import lax
from jax.sharding import PartitionSpec as P

S = 128
C = 32
CZ = 128


def on_device(left_act, right_act, out_weight, out_bias, pair_grad):
    factor = 1.0 / S
    tile_rows = left_act.shape[0]
    tile_cols = right_act.shape[0]
    first_total = tile_rows * lax.axis_size("row")
    left_whole = lax.all_gather(left_act, "col", axis=1, tiled=True)
    left_tiles = left_whole.reshape(tile_rows, S, C)
    right_whole = lax.all_gather(right_act, "row", axis=1, tiled=True)
    right_tiles = right_whole.reshape(tile_cols, S, C)
    outer_sum = jnp.einsum(
        "isc,jsd->ijcd", left_tiles, right_tiles, preferred_element_type=jnp.float32
    )
    outer = (outer_sum * factor).astype(jnp.bfloat16).reshape(tile_rows * tile_cols, C * C)
    pre = jnp.dot(outer, out_weight, preferred_element_type=jnp.float32) + out_bias
    sigmoid_pre = jax.nn.sigmoid(pre)
    pair_out = (pre * sigmoid_pre).astype(jnp.bfloat16).reshape(tile_rows, tile_cols, CZ)
    slope = sigmoid_pre * (1.0 + pre * (1.0 - sigmoid_pre))
    dpre = (pair_grad.reshape(tile_rows * tile_cols, CZ).astype(jnp.float32) * slope).astype(
        jnp.bfloat16
    )
    weight_term = lax.dot_general(
        outer, dpre, (((0,), (0,)), ((), ())), preferred_element_type=jnp.float32
    )
    bias_term = jnp.sum(dpre.astype(jnp.float32), axis=0)
    weight_grad, bias_grad = lax.psum(
        (weight_term / first_total, bias_term / first_total), ("row", "col")
    )
    douter = lax.dot_general(
        dpre, out_weight, (((1,), (1,)), ((), ())), preferred_element_type=jnp.float32
    )
    douter = douter.astype(jnp.bfloat16).reshape(tile_rows, tile_cols, C, C)
    right_term = (
        jnp.einsum("ijcd,isc->jsd", douter, left_tiles, preferred_element_type=jnp.float32) * factor
    )
    right_grad = lax.psum_scatter(
        right_term.reshape(tile_cols, S * C), "row", scatter_dimension=1, tiled=True
    )
    left_term = (
        jnp.einsum("ijcd,jsd->isc", douter, right_tiles, preferred_element_type=jnp.float32)
        * factor
    )
    left_grad = lax.psum_scatter(
        left_term.reshape(tile_rows, S * C), "col", scatter_dimension=1, tiled=True
    )
    return (pair_out, left_grad, right_grad, weight_grad, bias_grad)


def solution(mesh):
    in_specs = (P("row", "col"), P("col", "row"), P(), P(), P("row", "col", None))
    out_specs = (P("row", "col", None), P("row", "col"), P("col", "row"), P(), P())
    return jax.shard_map(
        on_device, mesh=mesh, in_specs=in_specs, out_specs=out_specs, check_vma=False
    )
```

profile of v0, /device:TPU:1, one launch (start us, length us, event | category | flops | bytes accessed | tf_op | source)
XLA Modules:
  0.0 520.6 jit_solution(513587875001228488)
XLA Ops:
  7.2 0.0 copy-start
  7.2 0.0 all-gather.2.cloned.1.call-start
  7.2 1.5 copy.13
  8.7 0.0 all-gather.2.cloned.1.call-update
  8.8 0.0 reduce-scatter.5.cloned.1.call-start
  8.8 24.2 %all_gather.7 = bf16[32,4096]{1,0:T(8,128)(2,1)S(1)} all-gather(bf16[32,512]{1,0:T(8,128)(2,1)} %param.5), channel_id=1, replica_groups=mesh['row'=32,'col'=8] {'col'}, dimensions={1}, use_global_device_ids=true | all-gather | bytes 294912 | tf_op jit(solution)/shard_map/all_gather | solution.py:16
  33.0 0.8 reshape.36
  33.8 0.5 copy.30
  34.4 33.1 %all-gather.2.cloned.1.call-done = bf16[128,4096]{0,1:T(8,128)(2,1)} async-done(((bf16[128,128]{0,1:T(8,128)(2,1)}), bf16[128,4096]{0,1:T(8,128)(2,1)}) %all-gather.2.cloned.1.call-update) | async-done | bytes 1048592 | tf_op jit(solution)/shard_map/all_gather | solution.py:18
  67.4 6.9 %fusion.6 = bf16[32,128,32,32]{1,2,0,3:T(8,128)(2,1)} fusion(bf16[128,128,32,1]{0,2,1,3:T(8,128)(2,1)} %bitcast.64, bf16[32,128,32]{2,1,0:T(8,128)(2,1)S(1)} %reshape.36), kind=kOutput, calls=%fused_computation.8 | convolution fusion | flops 1082130432 | bytes 9699328 | tf_op jit(solution)/shard_map/isc,jsd->ijcd/dot_general | solution.py:20
  74.3 0.0 copy-start.2
  74.3 0.0 copy-start.3
  74.3 9.9 %copy.16 = bf16[32,128,32,32]{1,0,3,2:T(8,128)(2,1)} copy(bf16[32,128,32,32]{1,2,0,3:T(8,128)(2,1)} %fusion.6) | data formatting | bytes 16777216 | tf_op jit(solution)/shard_map/convert_element_type | solution.py:23
  84.2 0.0 copy-done
  84.2 0.0 copy-done.2
  84.2 0.0 copy-done.3
  84.2 13.4 %convert_reduce_fusion = (f32[128]{0:T(128)S(1)}, bf16[4096,128]{1,0:T(8,128)(2,1)S(1)}, bf16[4096,128]{1,0:T(8,128)(2,1)}) fusion(bf16[32,128,128]{2,1,0:T(8,128)(2,1)S(1)} %copy-done.2, f32[128]{0:T(128)S(1)} %copy-done.3, bf16[1024,128]{1,0:T(8,128)(2,1)S(1)} %copy-done, bf16[128,8,32,128]{3,2,1,0:T(8,128)(2,1)} %bitcast.61), kind=kOutput, calls=%fused_computation.14 | convolution fusion | flops 1081606016 | bytes 11797504 | tf_op jit(solution)/shard_map/dot_general | solution.py:24
  97.6 5.6 %convolution_convert_fusion = bf16[4096,1024]{1,0:T(8,128)(2,1)} fusion(bf16[4096,128]{1,0:T(8,128)(2,1)S(1)} %get-tuple-element.11, bf16[1024,128]{1,0:T(8,128)(2,1)S(1)} %copy-done), kind=kOutput, calls=%fused_computation.5 | convolution fusion | flops 1077936128 | bytes 9699328 | tf_op jit(solution)/shard_map/dot_general | solution.py:38
  103.2 11.3 %copy.17 = bf16[4096,1024]{0,1:T(8,128)(2,1)} copy(bf16[4096,1024]{1,0:T(8,128)(2,1)} %convolution_convert_fusion) | data formatting | bytes 16777216 | tf_op jit(solution)/shard_map/convert_element_type | solution.py:41
  114.5 9.4 %copy.37 = bf16[128,8,32,128]{3,2,1,0:T(8,128)(2,1)} copy(bf16[128,8,32,128]{3,1,2,0:T(8,128)(2,1)} %bitcast.59) | data formatting | bytes 16777216
  124.0 0.0 copy-start.1
  124.0 4.8 fusion.11
  128.8 2.6 copy.23
  131.3 0.0 reduce-scatter.5.cloned.1.call-update
  131.3 0.3 all-reduce.2.cloned.1.call-start
  131.6 0.0 copy-done.1
  131.6 1.0 copy.19
  132.6 6.6 %fusion.12 = f32[1024,128]{1,0:T(8,128)} fusion(bf16[4096,128]{1,0:T(8,128)(2,1)S(1)} %get-tuple-element.11, bf16[128,8,32,128]{3,2,1,0:T(8,128)(2,1)} %bitcast.62), kind=kOutput, calls=%fused_computation.17 | convolution fusion | flops 1073872896 | bytes 9961472 | tf_op jit(solution)/shard_map/dot_general | solution.py:31
  139.2 0.0 all-reduce.2.cloned.1.call-update
  139.2 0.0 reduce-scatter.3.cloned.1.call-start
  139.3 5.8 %fusion.15 = f32[32,32,128,1]{2,0,3,1:T(8,128)S(1)} fusion(bf16[32,128,32,32]{1,0,3,2:T(8,128)(2,1)} %bitcast.58, bf16[128,128,32]{1,0,2:T(8,128)(2,1)S(1)} %copy.19), kind=kOutput, calls=%fused_computation.18 | convolution fusion | flops 1073741824 | bytes 9961472 | tf_op jit(solution)/shard_map/ijcd,jsd->isc/dot_general | solution.py:49
  145.1 0.3 fusion.18
  145.4 0.6 copy.20
  146.0 1.7 reshape.40
  147.8 0.0 reduce-scatter.3.cloned.1.call-update
  147.8 75.8 %psum.15 = f32[128]{0:T(128)} all-reduce(f32[128]{0:T(128)S(1)} %broadcast_multiply_fusion), channel_id=1, replica_groups=mesh['row'=32,'col'=8] {'row','col'}, use_global_device_ids=true, to_apply=%region_4.0 | all-reduce | flops 128 | bytes 1024 | tf_op jit(solution)/shard_map/psum | solution.py:35
  223.6 0.0 reduce-scatter.5.cloned.1.call-done
  223.6 1.6 copy.24
  225.2 248.6 %all-reduce.2.cloned.1.call-done = f32[1024,128]{1,0:T(8,128)} async-done(((f32[1024,128]{1,0:T(8,128)}), f32[1024,128]{1,0:T(8,128)}) %all-reduce.2.cloned.1.call-update) | async-done | bytes 524304 | tf_op jit(solution)/shard_map/psum | solution.py:35
  473.7 38.4 %reduce-scatter.3.cloned.1.call-done = f32[32,512]{1,0:T(8,128)} async-done(((f32[32,4096]{1,0:T(8,128)}), f32[32,512]{1,0:T(8,128)}) %reduce-scatter.3.cloned.1.call-update) | async-done | bytes 65552 | tf_op jit(solution)/shard_map/reduce_scatter | solution.py:52
  512.2 1.9 copy.56
  (1 shorter events, 0.0 us)
Async XLA Ops:
  7.2 77.1 %copy-start = (bf16[1024,128]{1,0:T(8,128)(2,1)S(1)}, bf16[1024,128]{1,0:T(8,128)(2,1)}, u32[]{:S(2)}) copy-start(bf16[1024,128]{1,0:T(8,128)(2,1)} %param.7) | copy-start | bytes 786436
  7.2 60.2 %all-gather.2.cloned.1.call-start = ((), (), s32[]{:S(2)}) async-start(), calls=%async_computation.2 | async-start | bytes 1081344 | tf_op jit(solution)/shard_map/all_gather | solution.py:18
  8.8 214.8 %reduce-scatter.5.cloned.1.call-start = ((), (), s32[]{:S(2)}) async-start(), calls=%async_computation.4 | async-start | bytes 2162688 | tf_op jit(solution)/shard_map/reduce_scatter | solution.py:45
  74.3 9.9 %copy-start.2 = (bf16[32,128,128]{2,1,0:T(8,128)(2,1)S(1)}, bf16[32,128,128]{2,1,0:T(8,128)(2,1)}, u32[]{:S(2)}) copy-start(bf16[32,128,128]{2,1,0:T(8,128)(2,1)} %param.9) | copy-start | bytes 3145732
  74.3 9.9 %copy-start.3 = (f32[128]{0:T(128)S(1)}, f32[128]{0:T(128)}, u32[]{:S(2)}) copy-start(f32[128]{0:T(128)} %param.8) | copy-start | bytes 1540
  124.0 7.6 %copy-start.1 = (bf16[128,4096]{0,1:T(8,128)(2,1)S(1)}, bf16[128,4096]{0,1:T(8,128)(2,1)}, u32[]{:S(2)}) copy-start(bf16[128,4096]{0,1:T(8,128)(2,1)} %all-gather.2.cloned.1.call-done) | copy-start | bytes 3145732
  131.3 342.4 %all-reduce.2.cloned.1.call-start = ((), (), s32[]{:S(2)}) async-start(), calls=%async_computation.5 | async-start | bytes 1048576 | tf_op jit(solution)/shard_map/psum | solution.py:35
  139.2 372.9 %reduce-scatter.3.cloned.1.call-start = ((), (), s32[]{:S(2)}) async-start(), calls=%async_computation.3 | async-start | bytes 589824 | tf_op jit(solution)/shard_map/reduce_scatter | solution.py:52
Sparse Core Ops, SparseCore 0:
  11.1 56.2 all-gather.1
  131.5 86.8 reduce-scatter.4
  223.8 249.8 all-reduce.1
  476.7 35.4 reduce-scatter.2
where the time goes:
time: 525 us; the launch traced here: 521 us
  waiting for transfers between devices  320 us (61%)
  blocking collectives  100 us (19%)
  matrix products  43 us (8%)
  local copies, waits for them, and re-layouts  42.9 us (8%)
  between operations  13.8 us (3%)
    psum x1, waiting for transfers between devices, on_device(): lax.psum((weight_term / first_total, bias_term / first_total), ('row', 'c...  249 us
    psum x1, blocking collectives, on_device(): lax.psum((weight_term / first_total, bias_term / first_total), ('row', 'c...  75.8 us
    reduce_scatter x1, waiting for transfers between devices, on_device(): lax.psum_scatter(left_term.reshape(tile_rows, S * C), 'col', scatter_dime...  38.4 us
    all_gather x1, waiting for transfers between devices, on_device(): right_whole = lax.all_gather(right_act, 'row', axis=1, tiled=True)  33.1 us
    all_gather x1, blocking collectives, on_device(): left_whole = lax.all_gather(left_act, 'col', axis=1, tiled=True)  24.2 us
    unnamed x12, local copies, waits for them, and re-layouts  14.4 us
    dot_general x1, matrix products, on_device(): jnp.dot(outer, out_weight, preferred_element_type=jnp.float32) + out_bias  13.4 us
    convert_element_type x1, local copies, waits for them, and re-layouts, on_device(): douter = douter.astype(jnp.bfloat16).reshape(tile_rows, tile_cols, C, C)  11.3 us
  transfers between devices with their start and end apart: 4, of which 3 were waited for; matrix products, arithmetic and copies ran while one was open for 4% of the time, Pallas kernels for 0%

commit v1 on v0

v1 whole, which is shorter than its diff:
```python
import jax
import jax.numpy as jnp
from jax import lax
from jax.experimental import pallas as pl
from jax.experimental.pallas import tpu as pltpu
from jax.sharding import Mesh, PartitionSpec as P

S = 128
C = 32
CZ = 128
CC = C * C
TI = 32
TJ = 128
BF = jnp.bfloat16
F32 = jnp.float32
AXES = ("h", "x", "c", "l", "y")
ROW = ("h", "x", "c")
CHIP = ("h", "x")
COL = ("l", "y")
COST = pl.CostEstimate(flops=6 << 30, transcendentals=0, bytes_accessed=4 << 20)
NN = (((1,), (0,)), ((), ()))
NT = (((1,), (1,)), ((), ()))


def forward_kernel(
    pos_ref, a_ref, mine_ref, other_ref, wt_ref, bias_ref, g_ref,
    po_out, dp_out, b_out, wg_ref,
    at, rows, x, wsum, po_ref, dp_ref, b_ref, sems,
):
    first = pos_ref[2] == 0
    for k in range(4):
        for m in range(4):
            t = ((pos_ref[0] + 4 - m) % 4) * 4 + (pos_ref[1] + 4 - k) % 4
            u = mine_ref[k, m].astype(F32)
            v = other_ref[k, m].astype(F32)
            rows[pl.ds(pl.multiple_of(t * 8, 8), 8), :] = jnp.concatenate(
                [jnp.where(first, u, v), jnp.where(first, v, u)], axis=0
            )
    b_ref[...] = rows[...].astype(BF)
    b_copy = pltpu.make_async_copy(b_ref, b_out, sems.at[0])
    b_copy.start()
    at[...] = a_ref[...].astype(F32).T.astype(BF)
    for n in range(C // 2):
        o = lax.dot_general(
            at[...], b_ref[:, n * 256 : (n + 1) * 256], NN, preferred_element_type=F32
        ).astype(BF)
        for e in range(2):
            d = 2 * n + e
            for i in range(TI):
                x[d * C : (d + 1) * C, i * TJ : (i + 1) * TJ] = o[
                    i * C : (i + 1) * C, e * TJ : (e + 1) * TJ
                ]
    bias = bias_ref[...]
    total = jnp.zeros((8, CZ), F32)
    for q in range(8):
        pre_t = lax.dot_general(
            wt_ref[...], x[:, q * 512 : (q + 1) * 512], NN, preferred_element_type=F32
        )
        pre = pre_t.T + bias
        sig = 1.0 / (1.0 + jnp.exp(-pre))
        po_ref[q * 512 : (q + 1) * 512, :] = (pre * sig).astype(BF)
        slope = sig * (1.0 + pre * (1.0 - sig))
        dpre = (g_ref[q * 512 : (q + 1) * 512, :].astype(F32) * slope).astype(BF)
        dp_ref[q * 512 : (q + 1) * 512, :] = dpre
        total = total + jnp.sum(dpre.astype(F32).reshape(64, 8, CZ), axis=0)
    dp_copy = pltpu.make_async_copy(dp_ref, dp_out, sems.at[1])
    dp_copy.start()
    po_copy = pltpu.make_async_copy(po_ref, po_out, sems.at[2])
    po_copy.start()
    for m in range(4):
        w = lax.dot_general(
            x[m * 256 : (m + 1) * 256, :], dp_ref[...], NN, preferred_element_type=F32
        )
        for k in range(8):
            wsum[pl.ds(m * 8 + k, C, stride=C), :] = w[k * C : (k + 1) * C, :]
    row = jnp.broadcast_to(jnp.sum(total, axis=0, keepdims=True), (8, CZ))
    for c in range(C):
        wg_ref[c, :, :] = jnp.concatenate([wsum[c * C : (c + 1) * C, :], row], axis=0).astype(BF)
    b_copy.wait()
    dp_copy.wait()
    po_copy.wait()


def backward_kernel(
    pos_ref, dp_in, b_in, w_ref, a_ref, rm_ref, ro_ref, l_ref, dd, dp_ref, b_ref, sems
):
    first = pos_ref[2] == 0
    dp_copy = pltpu.make_async_copy(dp_in, dp_ref, sems.at[0])
    dp_copy.start()
    b_copy = pltpu.make_async_copy(b_in, b_ref, sems.at[1])
    b_copy.start()
    dp_copy.wait()
    for q in range(TI // 2):
        g = lax.dot_general(
            w_ref[...], dp_ref[q * 256 : (q + 1) * 256, :], NT, preferred_element_type=F32
        ).astype(BF)
        for e in range(2):
            i = 2 * q + e
            for d in range(C):
                dd[i * C : (i + 1) * C, d * TJ : (d + 1) * TJ] = g[
                    d * C : (d + 1) * C, e * TJ : (e + 1) * TJ
                ]
    for n in range(8):
        r = lax.dot_general(
            a_ref[...], dd[:, n * 512 : (n + 1) * 512], NN, preferred_element_type=F32
        )
        for t in range(16):
            k = (t % 4 + 4 - pos_ref[1]) % 4
            m = (t // 4 + 4 - pos_ref[0]) % 4
            u = r[8 * t : 8 * t + 4, :]
            v = r[8 * t + 4 : 8 * t + 8, :]
            rm_ref[k, m, :, n * 512 : (n + 1) * 512] = jnp.where(first, u, v)
            ro_ref[k, m, :, n * 512 : (n + 1) * 512] = jnp.where(first, v, u).astype(BF)
    b_copy.wait()
    for m in range(4):
        t = lax.dot_general(
            dd[m * 256 : (m + 1) * 256, :], b_ref[...], NT, preferred_element_type=F32
        )
        l_ref[:, m * 256 : (m + 1) * 256] = (t.T * (1.0 / S)).astype(BF)


SCALARS = pl.BlockSpec(memory_space=pltpu.SMEM)
FAR = pl.BlockSpec(memory_space=pltpu.HBM)
WHOLE = pl.BlockSpec(memory_space=pltpu.VMEM)


def forward_call(*args):
    return pl.pallas_call(
        forward_kernel,
        in_specs=[SCALARS] + [WHOLE] * 6,
        out_specs=(FAR, FAR, FAR, WHOLE),
        out_shape=(
            jax.ShapeDtypeStruct((TI * TJ, CZ), BF),
            jax.ShapeDtypeStruct((TI * TJ, CZ), BF),
            jax.ShapeDtypeStruct((S, C * TJ), BF),
            jax.ShapeDtypeStruct((C, C + 8, CZ), BF),
        ),
        scratch_shapes=[
            pltpu.VMEM((TI * C, S), BF),
            pltpu.VMEM((S, C * TJ), F32),
            pltpu.VMEM((CC, TI * TJ), BF),
            pltpu.VMEM((CC, CZ), F32),
            pltpu.VMEM((TI * TJ, CZ), BF),
            pltpu.VMEM((TI * TJ, CZ), BF),
            pltpu.VMEM((S, C * TJ), BF),
            pltpu.SemaphoreType.DMA((3,)),
        ],
        compiler_params=pltpu.CompilerParams(vmem_limit_bytes=40 << 20),
        cost_estimate=COST,
        name="forward",
    )(*args)


def backward_call(*args):
    return pl.pallas_call(
        backward_kernel,
        in_specs=[SCALARS, FAR, FAR, WHOLE, WHOLE],
        out_specs=(WHOLE,) * 3,
        out_shape=(
            jax.ShapeDtypeStruct((4, 4, 4, C * TJ), F32),
            jax.ShapeDtypeStruct((4, 4, 4, C * TJ), BF),
            jax.ShapeDtypeStruct((S, TI * C), BF),
        ),
        scratch_shapes=[
            pltpu.VMEM((TI * C, C * TJ), BF),
            pltpu.VMEM((TI * TJ, CZ), BF),
            pltpu.VMEM((S, C * TJ), BF),
            pltpu.SemaphoreType.DMA((2,)),
        ],
        compiler_params=pltpu.CompilerParams(vmem_limit_bytes=40 << 20),
        cost_estimate=COST,
        name="backward",
    )(*args)


def shift(x, axis, k):
    return lax.ppermute(x, axis, [(i, (i + k) % 4) for i in range(4)])


def gather4(x, axis):
    return jnp.stack([x] + [shift(x, axis, k) for k in (1, 2, 3)])


def reduce4(x, axis):
    return x[0].astype(F32) + sum(shift(x[k], axis, k).astype(F32) for k in (1, 2, 3))


def swap(x):
    return lax.ppermute(x, "c", [(0, 1), (1, 0)])


def exchange(x, axes):
    return lax.all_to_all(x, axes, split_axis=0, concat_axis=0, tiled=True)


def spread(x, axes, n):
    return exchange(jnp.broadcast_to(x[None], (n,) + x.shape), axes)


def on_device(left_act, right_act, out_weight, out_bias, pair_grad):
    pos = jnp.stack([lax.axis_index("h"), lax.axis_index("x"), lax.axis_index("c")])
    mine = gather4(gather4(right_act.T.reshape(4, C * TJ), "h"), "x")
    left = (left_act * (1.0 / S)).astype(BF).reshape(TI, 16, C).transpose(1, 0, 2)
    a = spread(left.reshape(16, TI * C), COL, 8).reshape(S, TI * C)
    mine, a = lax.optimization_barrier((mine, a))
    other = swap(mine)
    w = out_weight.reshape(C, C, CZ).transpose(1, 0, 2).reshape(CC, CZ)
    pair_out, dp, b, wg = forward_call(
        pos, a, mine, other, w.T, out_bias.reshape(1, CZ), pair_grad.reshape(TI * TJ, CZ)
    )
    wg = exchange(wg, ROW)
    r_own, r_oth, l = backward_call(pos, dp, b, w, a)
    moved = [swap(r_oth[k]) for k in range(4)]
    wg, l, _ = lax.optimization_barrier((wg, l, moved))
    wg = jnp.sum(wg.astype(F32), axis=0).reshape(5, TI * C)
    high = lax.reduce_precision(wg, 8, 7)
    pair = jnp.concatenate([high, wg - high, jnp.zeros((6, TI * C), F32)], axis=0).astype(BF)
    both = exchange(
        jnp.concatenate(
            [l.reshape(8, 16, TI * C), jnp.broadcast_to(pair[None], (8, 16, TI * C))], axis=1
        ),
        COL,
    )
    both = jnp.sum(both.astype(F32), axis=0)
    left_grad = both[:16].reshape(16, TI, C).transpose(1, 0, 2).reshape(TI, 16 * C)
    wg = (both[16:21] + both[21:26]).reshape(C + 8, CZ) * (1.0 / (TI * 32))
    bias_grad = wg[C]
    full = spread(wg[:C].astype(BF), ROW, 32)
    full, left_grad, bias_grad = lax.optimization_barrier((full, left_grad, bias_grad))
    weight_grad = full.astype(F32).reshape(CC, CZ)
    r = [(r_own[k] + moved[k].astype(F32)).astype(BF) for k in range(4)]
    right_sum = reduce4(reduce4(r, "x"), "h")
    right_grad = right_sum.reshape(4 * C, TJ).T
    return (
        pair_out.reshape(TI, TJ, CZ),
        left_grad,
        right_grad,
        weight_grad,
        bias_grad,
    )


def solution(mesh):
    fine = Mesh(mesh.devices.reshape(4, 4, 2, 2, 4), AXES)
    in_specs = (P(ROW, COL), P(COL, ROW), P(), P(), P(ROW, COL, None))
    out_specs = (P(ROW, COL, None), P(ROW, COL), P(COL, ROW), P(), P())
    return jax.shard_map(
        on_device, mesh=fine, in_specs=in_specs, out_specs=out_specs, check_vma=False
    )
```

time: 525 us -> 106 us (0.20)
  waiting for transfers between devices: 320 us -> 33.6 us
  blocking collectives: 100 us -> 0 us
  starting transfers between devices: 0.38 us -> 46 us
  matrix products: 43 us -> 0 us
  local copies, waits for them, and re-layouts: 42.9 us -> 6.3 us
  Pallas kernels: 0 us -> 16.1 us
  between operations: 13.8 us -> 0.92 us
    psum x1 -> x0, waiting for transfers between devices: 249 us -> none  [on_device(): lax.psum((weight_term / first_total, bias_term / first_total), ('row', 'c...]
    psum x1 -> x0, blocking collectives: 75.8 us -> none  [on_device(): lax.psum((weight_term / first_total, bias_term / first_total), ('row', 'c...]
    dot_general x6 -> x0, matrix products: 43 us -> none  [the longest x1 13.4 us: on_device(): jnp.dot(outer, out_weight, preferred_element_type=jnp.float32) + out_bias]
    reduce_scatter x2 -> x0, waiting for transfers between devices: 38.4 us -> none  [the longest x1 38.4 us: on_device(): lax.psum_scatter(left_term.reshape(tile_rows, S * C), 'col', scatter_dime...]
    all_gather x1 -> x0, waiting for transfers between devices: 33.1 us -> none  [on_device(): right_whole = lax.all_gather(right_act, 'row', axis=1, tiled=True)]
    ppermute x0 -> x17, starting transfers between devices: none -> 26.4 us  [the longest x12 21.8 us: shift(): return lax.ppermute(x, axis, [(i, (i + k) % 4) for i in range(4)])]
    all_to_all x0 -> x4, waiting for transfers between devices: none -> 26.4 us  [exchange(): return lax.all_to_all(x, axes, split_axis=0, concat_axis=0, tiled=True)]
    all_gather x1 -> x0, blocking collectives: 24.2 us -> none  [on_device(): left_whole = lax.all_gather(left_act, 'col', axis=1, tiled=True)]
  transfers between devices with their start and end apart: 4 -> 21, of which waited for: 3 -> 7; matrix products, arithmetic and copies ran while one was open for 4% -> 6% of each run, Pallas kernels for 0% -> 0%
where the time goes in v1:
time: 106 us
  starting transfers between devices  46 us (43%)
  waiting for transfers between devices  33.6 us (32%)
  Pallas kernels  16.1 us (15%)
  local copies, waits for them, and re-layouts  6.3 us (6%)
  other arithmetic  3.1 us (3%)
    all_to_all x4, waiting for transfers between devices, exchange(): return lax.all_to_all(x, axes, split_axis=0, concat_axis=0, tiled=True)  26.4 us
    ppermute x12, starting transfers between devices, shift(): return lax.ppermute(x, axis, [(i, (i + k) % 4) for i in range(4)])  21.8 us
    all_to_all x4, starting transfers between devices, exchange(): return lax.all_to_all(x, axes, split_axis=0, concat_axis=0, tiled=True)  19.5 us
    pallas_call x1, Pallas kernels, forward_call(): pl.pallas_call(forward_kernel, in_specs=[SCALARS] + [WHOLE] * 6, out_spec...  9.1 us
    pallas_call x1, Pallas kernels, backward_call(): pl.pallas_call(backward_kernel, in_specs=[SCALARS, FAR, FAR, WHOLE, WHOLE...  7 us
    ppermute x12, waiting for transfers between devices, shift(): return lax.ppermute(x, axis, [(i, (i + k) % 4) for i in range(4)])  6 us
    ppermute x5, starting transfers between devices, swap(): return lax.ppermute(x, 'c', [(0, 1), (1, 0)])  4.62 us
  transfers between devices with their start and end apart: 21, of which 7 were waited for; matrix products, arithmetic and copies ran while one was open for 6% of the time, Pallas kernels for 0%

profile of v1, /device:TPU:1, one launch (start us, length us, event | category | flops | bytes accessed | tf_op | source)
XLA Modules:
  0.0 106.0 jit_solution(2211659116974986019)
XLA Ops:
  0.6 0.9 copy.21
  1.5 6.9 %collective-permute-start.2 = (bf16[4,4096]{1,0:T(4,128)(2,1)S(1)}, bf16[4,4096]{1,0:T(4,128)(2,1)S(1)}, u32[]{:S(2)}, u32[]{:S(2)}) collective-permute-start(bf16[4,4096]{1,0:T(4,128)(2,1)S(1)} %reshape.81), channel_id=1, source_target_pairs={{0,192},{64,0},{128,64},{192,128},{1,193},{65,1},{129,65},{193,129... | collective-permute-start | bytes 98312 | tf_op jit(solution)/shard_map/ppermute | solution.py:177
  8.5 1.0 collective-permute-start.1
  9.4 2.3 %collective-permute-start = (bf16[4,4096]{1,0:T(4,128)(2,1)S(1)}, bf16[4,4096]{1,0:T(4,128)(2,1)S(1)}, u32[]{:S(2)}, u32[]{:S(2)}) collective-permute-start(bf16[4,4096]{1,0:T(4,128)(2,1)S(1)} %reshape.81), channel_id=1, source_target_pairs={{0,64},{64,128},{128,192},{192,0},{1,65},{65,129},{129,193},{193,1... | collective-permute-start | bytes 98312 | tf_op jit(solution)/shard_map/ppermute | solution.py:177
  11.7 0.1 reshape.82
  11.9 0.2 broadcast_in_dim.10
  12.1 0.7 broadcast_in_dim.11
  12.8 4.6 %all-to-all-start = ((bf16[8,16,1024]{2,1,0:T(8,128)(2,1)}), bf16[8,16,1024]{2,1,0:T(8,128)(2,1)S(1)}, u32[]{:S(2)}, u32[]{:S(2)}) async-start(bf16[8,16,1024]{2,1,0:T(8,128)(2,1)} %broadcast_in_dim.11), calls=%async_computation | async-start | bytes 524288 | tf_op jit(solution)/shard_map/all_to_all | solution.py:193
  17.5 0.1 pad_maximum_fusion.2
  17.6 2.6 %collective-permute-start.5 = (bf16[4,4,4096]{2,1,0:T(4,128)(2,1)S(1)}, bf16[4,4,4096]{2,1,0:T(4,128)(2,1)S(1)}, u32[]{:S(2)}, u32[]{:S(2)}) collective-permute-start(bf16[4,4,4096]{2,1,0:T(4,128)(2,1)S(1)} %pad_maximum_fusion.2), channel_id=1, source_target_pairs={{0,48},{16,0},{32,16},{48,32},{1,49},{17,1},{33,17},{49,33},{2,50}... | collective-permute-start | bytes 393224 | tf_op jit(solution)/shard_map/ppermute | solution.py:177
  20.2 0.5 collective-permute-start.4
  20.7 0.6 collective-permute-start.3
  21.4 1.2 %collective-permute-done.5 = bf16[4,4,4096]{2,1,0:T(4,128)(2,1)S(1)} collective-permute-done((bf16[4,4,4096]{2,1,0:T(4,128)(2,1)S(1)}, bf16[4,4,4096]{2,1,0:T(4,128)(2,1)S(1)}, u32[]{:S(2)}, u32[]{:S(2)}) %collective-permute-start.5) | collective-permute-done | bytes 131104 | tf_op jit(solution)/shard_map/ppermute | solution.py:177
  22.6 3.2 %collective-permute-done.4 = bf16[4,4,4096]{2,1,0:T(4,128)(2,1)S(1)} collective-permute-done((bf16[4,4,4096]{2,1,0:T(4,128)(2,1)S(1)}, bf16[4,4,4096]{2,1,0:T(4,128)(2,1)S(1)}, u32[]{:S(2)}, u32[]{:S(2)}) %collective-permute-start.4) | collective-permute-done | bytes 131104 | tf_op jit(solution)/shard_map/ppermute | solution.py:177
  25.8 1.6 %collective-permute-done.3 = bf16[4,4,4096]{2,1,0:T(4,128)(2,1)S(1)} collective-permute-done((bf16[4,4,4096]{2,1,0:T(4,128)(2,1)S(1)}, bf16[4,4,4096]{2,1,0:T(4,128)(2,1)S(1)}, u32[]{:S(2)}, u32[]{:S(2)}) %collective-permute-start.3) | collective-permute-done | bytes 131104 | tf_op jit(solution)/shard_map/ppermute | solution.py:177
  27.4 0.5 pad_maximum_fusion.mine_ref
  27.9 3.1 %collective-permute-start.6 = (bf16[4,4,4,4096]{3,2,1,0:T(4,128)(2,1)S(1)}, bf16[4,4,4,4096]{3,2,1,0:T(4,128)(2,1)S(1)}, u32[]{:S(2)}, u32[]{:S(2)}) collective-permute-start(bf16[4,4,4,4096]{3,2,1,0:T(4,128)(2,1)S(1)} %pad_maximum_fusion.mine_ref), channel_id=1, source_target_pairs={{0,8},{8,0},{1,9},{9,1},{2,10},{10,2},{3,11},{11,3},{4,12},{12,4},... | collective-permute-start | bytes 1572872 | tf_op jit(solution)/shard_map/ppermute | solution.py:189
  31.1 0.1 copy.25.wt_ref
  31.3 1.2 %collective-permute-done.6.other_ref = bf16[4,4,4,4096]{3,2,1,0:T(4,128)(2,1)S(1)} collective-permute-done((bf16[4,4,4,4096]{3,2,1,0:T(4,128)(2,1)S(1)}, bf16[4,4,4,4096]{3,2,1,0:T(4,128)(2,1)S(1)}, u32[]{:S(2)}, u32[]{:S(2)}) %collective-permute-start.6) | collective-permute-done | bytes 524320 | tf_op jit(solution)/shard_map/ppermute | solution.py:189
  32.5 0.7 copy-done.1
  33.2 9.1 %forward.1 = (bf16[4096,128]{1,0:T(8,128)(2,1)}, bf16[4096,128]{1,0:T(8,128)(2,1)S(1)}, bf16[128,4096]{1,0:T(8,128)(2,1)S(1)}, bf16[32,40,128]{2,1,0:T(8,128)(2,1)}) custom-call(s32[3]{0:T(128)S(1)} %pad_add_fusion.pos_ref, bf16[128,1024]{1,0:T(8,128)(2,1)S(1)} %bitcast.71, bf16[4,4,4,4096]{3,2,1,0:T(4,128)(2,1)S(1)} %pad_maximum_fusion.mine_ref, ...), custom_call_target="tpu_custom_call" | custom-call | flops 6442450944 | bytes 4194304 | tf_op jit(solution)/shard_map/forward/pallas_call | solution.py:128
  42.3 7.0 %backward.1 = (f32[4,4,4,4096]{3,2,1,0:T(4,128)S(1)}, bf16[4,4,4,4096]{3,2,1,0:T(4,128)(2,1)S(1)}, bf16[128,1024]{1,0:T(8,128)(2,1)S(1)}) custom-call(s32[3]{0:T(128)S(1)} %pad_add_fusion.pos_ref, bf16[4096,128]{1,0:T(8,128)(2,1)S(1)} %get-tuple-element.23.dp_in, bf16[128,4096]{1,0:T(8,128)(2,1)S(1)} %get-tuple-element.24.b_in, ...), custom_call_target="tpu_custom_call" | custom-call | flops 6442450944 | bytes 4194304 | tf_op jit(solution)/shard_map/backward/pallas_call | solution.py:155
  49.3 0.2 slice_bitcast_fusion
  49.5 0.7 collective-permute-start.8
  50.2 0.1 collective-permute-start.9
  50.3 0.4 collective-permute-start.10
  50.8 4.5 %all-to-all-start.1 = ((bf16[32,40,128]{2,1,0:T(8,128)(2,1)}), bf16[32,40,128]{2,1,0:T(8,128)(2,1)S(1)}, u32[]{:S(2)}, u32[]{:S(2)}) async-start(bf16[32,40,128]{2,1,0:T(8,128)(2,1)} %get-tuple-element.22), calls=%async_computation.1 | async-start | bytes 655360 | tf_op jit(solution)/shard_map/all_to_all | solution.py:193
  55.3 0.3 collective-permute-start.7
  55.6 0.2 fusion.2
  55.9 2.8 %collective-permute-start.13 = (bf16[4,4,4096]{2,1,0:T(4,128)(2,1)S(1)}, bf16[4,4,4096]{2,1,0:T(4,128)(2,1)S(1)}, u32[]{:S(2)}, u32[]{:S(2)}) collective-permute-start(bf16[4,4,4096]{2,1,0:T(4,128)(2,1)S(1)} %get-tuple-element.34), channel_id=1, source_target_pairs={{0,48},{16,0},{32,16},{48,32},{1,49},{17,1},{33,17},{49,33},{2,50}... | collective-permute-start | bytes 393224 | tf_op jit(solution)/shard_map/ppermute | solution.py:177
  58.7 0.6 collective-permute-start.12
  59.2 0.6 collective-permute-start.11
  59.8 9.9 %all-to-all-done.1 = bf16[32,40,128]{2,1,0:T(8,128)(2,1)S(1)} async-done(((bf16[32,40,128]{2,1,0:T(8,128)(2,1)}), bf16[32,40,128]{2,1,0:T(8,128)(2,1)S(1)}, u32[]{:S(2)}, u32[]{:S(2)}) %all-to-all-start.1) | async-done | bytes 327712 | tf_op jit(solution)/shard_map/all_to_all | solution.py:193
  69.9 0.8 pad_maximum_fusion.1
  70.8 5.3 %all-to-all-start.2 = ((bf16[8,32,1024]{2,1,0:T(8,128)(2,1)}), bf16[8,32,1024]{2,1,0:T(8,128)(2,1)S(1)}, u32[]{:S(2)}, u32[]{:S(2)}) async-start(bf16[8,32,1024]{2,1,0:T(8,128)(2,1)} %pad_maximum_fusion.1), calls=%async_computation.2 | async-start | bytes 1048576 | tf_op jit(solution)/shard_map/all_to_all | solution.py:193
  76.1 0.1 add_add_fusion
  76.3 1.1 %collective-permute-start.16 = (f32[4,4096]{1,0:T(4,128)S(1)}, f32[4,4096]{1,0:T(4,128)S(1)}, u32[]{:S(2)}, u32[]{:S(2)}) collective-permute-start(f32[4,4096]{1,0:T(4,128)S(1)} %get-tuple-element.41), channel_id=1, source_target_pairs={{0,192},{64,0},{128,64},{192,128},{1,193},{65,1},{129,65},{193,129... | collective-permute-start | bytes 196616 | tf_op jit(solution)/shard_map/ppermute | solution.py:177
  77.4 1.3 %collective-permute-start.14 = (f32[4,4096]{1,0:T(4,128)S(1)}, f32[4,4096]{1,0:T(4,128)S(1)}, u32[]{:S(2)}, u32[]{:S(2)}) collective-permute-start(f32[4,4096]{1,0:T(4,128)S(1)} %get-tuple-element.42), channel_id=1, source_target_pairs={{0,64},{64,128},{128,192},{192,0},{1,65},{65,129},{129,193},{193,1... | collective-permute-start | bytes 196616 | tf_op jit(solution)/shard_map/ppermute | solution.py:177
  78.7 1.5 %collective-permute-start.15 = (f32[4,4096]{1,0:T(4,128)S(1)}, f32[4,4096]{1,0:T(4,128)S(1)}, u32[]{:S(2)}, u32[]{:S(2)}) collective-permute-start(f32[4,4096]{1,0:T(4,128)S(1)} %get-tuple-element.40), channel_id=1, source_target_pairs={{0,128},{64,192},{128,0},{192,64},{1,129},{65,193},{129,1},{193,65... | collective-permute-start | bytes 196616 | tf_op jit(solution)/shard_map/ppermute | solution.py:177
  80.3 5.9 %all-to-all-done.2 = bf16[8,32,1024]{2,1,0:T(8,128)(2,1)S(1)} async-done(((bf16[8,32,1024]{2,1,0:T(8,128)(2,1)}), bf16[8,32,1024]{2,1,0:T(8,128)(2,1)S(1)}, u32[]{:S(2)}, u32[]{:S(2)}) %all-to-all-start.2) | async-done | bytes 524320 | tf_op jit(solution)/shard_map/all_to_all | solution.py:193
  86.3 0.7 broadcast_in_dim.26
  87.1 5.1 %all-to-all-start.3 = ((bf16[32,32,128]{2,1,0:T(8,128)(2,1)}), bf16[32,32,128]{2,1,0:T(8,128)(2,1)S(1)}, u32[]{:S(2)}, u32[]{:S(2)}) async-start(bf16[32,32,128]{2,1,0:T(8,128)(2,1)} %broadcast_in_dim.26), calls=%async_computation.3 | async-start | bytes 524288 | tf_op jit(solution)/shard_map/all_to_all | solution.py:193
  92.3 0.7 copy.27
  93.2 0.2 copy.26
  93.3 0.8 reshape.92
  94.1 0.5 slice_bitcast_fusion.8
  94.6 10.5 %all-to-all-done.3 = bf16[32,32,128]{2,1,0:T(8,128)(2,1)S(1)} async-done(((bf16[32,32,128]{2,1,0:T(8,128)(2,1)}), bf16[32,32,128]{2,1,0:T(8,128)(2,1)S(1)}, u32[]{:S(2)}, u32[]{:S(2)}) %all-to-all-start.3) | async-done | bytes 262176 | tf_op jit(solution)/shard_map/all_to_all | solution.py:193
  105.1 0.8 bitcast_convert_fusion
  (45 shorter events, 1.0 us)
Async XLA Ops:
  1.5 10.2 %copy-start.3 = (bf16[32,512]{1,0:T(8,128)(2,1)S(1)}, bf16[32,512]{1,0:T(8,128)(2,1)}, u32[]{:S(2)}) copy-start(bf16[32,512]{1,0:T(8,128)(2,1)} %param.5) | copy-start | bytes 98308
  1.5 15.9 %collective-permute-start.2 = (bf16[4,4096]{1,0:T(4,128)(2,1)S(1)}, bf16[4,4096]{1,0:T(4,128)(2,1)S(1)}, u32[]{:S(2)}, u32[]{:S(2)}) collective-permute-start(bf16[4,4096]{1,0:T(4,128)(2,1)S(1)} %reshape.81), channel_id=1, source_target_pairs={{0,192},{64,0},{128,64},{192,128},{1,193},{65,1},{129,65},{193,129... | collective-permute-start | bytes 98312 | tf_op jit(solution)/shard_map/ppermute | solution.py:177
  8.5 9.0 %collective-permute-start.1 = (bf16[4,4096]{1,0:T(4,128)(2,1)S(1)}, bf16[4,4096]{1,0:T(4,128)(2,1)S(1)}, u32[]{:S(2)}, u32[]{:S(2)}) collective-permute-start(bf16[4,4096]{1,0:T(4,128)(2,1)S(1)} %reshape.81), channel_id=1, source_target_pairs={{0,128},{64,192},{128,0},{192,64},{1,129},{65,193},{129,1},{193,65... | collective-permute-start | bytes 98312 | tf_op jit(solution)/shard_map/ppermute | solution.py:177
  9.4 8.0 %collective-permute-start = (bf16[4,4096]{1,0:T(4,128)(2,1)S(1)}, bf16[4,4096]{1,0:T(4,128)(2,1)S(1)}, u32[]{:S(2)}, u32[]{:S(2)}) collective-permute-start(bf16[4,4096]{1,0:T(4,128)(2,1)S(1)} %reshape.81), channel_id=1, source_target_pairs={{0,64},{64,128},{128,192},{192,0},{1,65},{65,129},{129,193},{193,1... | collective-permute-start | bytes 98312 | tf_op jit(solution)/shard_map/ppermute | solution.py:177
  12.8 15.1 %all-to-all-start = ((bf16[8,16,1024]{2,1,0:T(8,128)(2,1)}), bf16[8,16,1024]{2,1,0:T(8,128)(2,1)S(1)}, u32[]{:S(2)}, u32[]{:S(2)}) async-start(bf16[8,16,1024]{2,1,0:T(8,128)(2,1)} %broadcast_in_dim.11), calls=%async_computation | async-start | bytes 524288 | tf_op jit(solution)/shard_map/all_to_all | solution.py:193
  17.6 5.0 %collective-permute-start.5 = (bf16[4,4,4096]{2,1,0:T(4,128)(2,1)S(1)}, bf16[4,4,4096]{2,1,0:T(4,128)(2,1)S(1)}, u32[]{:S(2)}, u32[]{:S(2)}) collective-permute-start(bf16[4,4,4096]{2,1,0:T(4,128)(2,1)S(1)} %pad_maximum_fusion.2), channel_id=1, source_target_pairs={{0,48},{16,0},{32,16},{48,32},{1,49},{17,1},{33,17},{49,33},{2,50}... | collective-permute-start | bytes 393224 | tf_op jit(solution)/shard_map/ppermute | solution.py:177
  20.2 5.6 %collective-permute-start.4 = (bf16[4,4,4096]{2,1,0:T(4,128)(2,1)S(1)}, bf16[4,4,4096]{2,1,0:T(4,128)(2,1)S(1)}, u32[]{:S(2)}, u32[]{:S(2)}) collective-permute-start(bf16[4,4,4096]{2,1,0:T(4,128)(2,1)S(1)} %pad_maximum_fusion.2), channel_id=1, source_target_pairs={{0,32},{16,48},{32,0},{48,16},{1,33},{17,49},{33,1},{49,17},{2,34}... | collective-permute-start | bytes 393224 | tf_op jit(solution)/shard_map/ppermute | solution.py:177
  20.7 6.7 %collective-permute-start.3 = (bf16[4,4,4096]{2,1,0:T(4,128)(2,1)S(1)}, bf16[4,4,4096]{2,1,0:T(4,128)(2,1)S(1)}, u32[]{:S(2)}, u32[]{:S(2)}) collective-permute-start(bf16[4,4,4096]{2,1,0:T(4,128)(2,1)S(1)} %pad_maximum_fusion.2), channel_id=1, source_target_pairs={{0,16},{16,32},{32,48},{48,0},{1,17},{17,33},{33,49},{49,1},{2,18}... | collective-permute-start | bytes 393224 | tf_op jit(solution)/shard_map/ppermute | solution.py:177
  21.3 9.7 %copy-start.2 = (bf16[1024,128]{1,0:T(8,128)(2,1)S(1)}, bf16[1024,128]{1,0:T(8,128)(2,1)}, u32[]{:S(2)}) copy-start(bf16[1024,128]{1,0:T(8,128)(2,1)} %param.7) | copy-start | bytes 786436
  27.4 5.1 %copy-start = (bf16[32,128,128]{2,1,0:T(8,128)(2,1)S(1)}, bf16[32,128,128]{2,1,0:T(8,128)(2,1)}, u32[]{:S(2)}) copy-start(bf16[32,128,128]{2,1,0:T(8,128)(2,1)} %param.9) | copy-start | bytes 3145732
  27.9 4.6 %collective-permute-start.6 = (bf16[4,4,4,4096]{3,2,1,0:T(4,128)(2,1)S(1)}, bf16[4,4,4,4096]{3,2,1,0:T(4,128)(2,1)S(1)}, u32[]{:S(2)}, u32[]{:S(2)}) collective-permute-start(bf16[4,4,4,4096]{3,2,1,0:T(4,128)(2,1)S(1)} %pad_maximum_fusion.mine_ref), channel_id=1, source_target_pairs={{0,8},{8,0},{1,9},{9,1},{2,10},{10,2},{3,11},{11,3},{4,12},{12,4},... | collective-permute-start | bytes 1572872 | tf_op jit(solution)/shard_map/ppermute | solution.py:189
  32.5 0.7 copy-start.1
  49.5 6.1 %collective-permute-start.8 = (bf16[4,4,4096]{2,1,0:T(4,128)(2,1)S(1)}, bf16[4,4,4096]{2,1,0:T(4,128)(2,1)S(1)}, u32[]{:S(2)}, u32[]{:S(2)}) collective-permute-start(bf16[4,4,4096]{2,1,0:T(4,128)(2,1)S(1)} %get-tuple-element.38), channel_id=1, source_target_pairs={{0,8},{8,0},{1,9},{9,1},{2,10},{10,2},{3,11},{11,3},{4,12},{12,4},... | collective-permute-start | bytes 393224 | tf_op jit(solution)/shard_map/ppermute | solution.py:189
  50.2 5.4 %collective-permute-start.9 = (bf16[4,4,4096]{2,1,0:T(4,128)(2,1)S(1)}, bf16[4,4,4096]{2,1,0:T(4,128)(2,1)S(1)}, u32[]{:S(2)}, u32[]{:S(2)}) collective-permute-start(bf16[4,4,4096]{2,1,0:T(4,128)(2,1)S(1)} %get-tuple-element.37), channel_id=1, source_target_pairs={{0,8},{8,0},{1,9},{9,1},{2,10},{10,2},{3,11},{11,3},{4,12},{12,4},... | collective-permute-start | bytes 393224 | tf_op jit(solution)/shard_map/ppermute | solution.py:189
  50.3 5.3 %collective-permute-start.10 = (bf16[4,4,4096]{2,1,0:T(4,128)(2,1)S(1)}, bf16[4,4,4096]{2,1,0:T(4,128)(2,1)S(1)}, u32[]{:S(2)}, u32[]{:S(2)}) collective-permute-start(bf16[4,4,4096]{2,1,0:T(4,128)(2,1)S(1)} %get-tuple-element.36), channel_id=1, source_target_pairs={{0,8},{8,0},{1,9},{9,1},{2,10},{10,2},{3,11},{11,3},{4,12},{12,4},... | collective-permute-start | bytes 393224 | tf_op jit(solution)/shard_map/ppermute | solution.py:189
  50.8 19.0 %all-to-all-start.1 = ((bf16[32,40,128]{2,1,0:T(8,128)(2,1)}), bf16[32,40,128]{2,1,0:T(8,128)(2,1)S(1)}, u32[]{:S(2)}, u32[]{:S(2)}) async-start(bf16[32,40,128]{2,1,0:T(8,128)(2,1)} %get-tuple-element.22), calls=%async_computation.1 | async-start | bytes 655360 | tf_op jit(solution)/shard_map/all_to_all | solution.py:193
  55.3 4.5 %collective-permute-start.7 = (bf16[4,4,4096]{2,1,0:T(4,128)(2,1)S(1)}, bf16[4,4,4096]{2,1,0:T(4,128)(2,1)S(1)}, u32[]{:S(2)}, u32[]{:S(2)}) collective-permute-start(bf16[4,4,4096]{2,1,0:T(4,128)(2,1)S(1)} %get-tuple-element.39), channel_id=1, source_target_pairs={{0,8},{8,0},{1,9},{9,1},{2,10},{10,2},{3,11},{11,3},{4,12},{12,4},... | collective-permute-start | bytes 393224 | tf_op jit(solution)/shard_map/ppermute | solution.py:189
  55.9 20.2 %collective-permute-start.13 = (bf16[4,4,4096]{2,1,0:T(4,128)(2,1)S(1)}, bf16[4,4,4096]{2,1,0:T(4,128)(2,1)S(1)}, u32[]{:S(2)}, u32[]{:S(2)}) collective-permute-start(bf16[4,4,4096]{2,1,0:T(4,128)(2,1)S(1)} %get-tuple-element.34), channel_id=1, source_target_pairs={{0,48},{16,0},{32,16},{48,32},{1,49},{17,1},{33,17},{49,33},{2,50}... | collective-permute-start | bytes 393224 | tf_op jit(solution)/shard_map/ppermute | solution.py:177
  58.7 17.4 %collective-permute-start.12 = (bf16[4,4,4096]{2,1,0:T(4,128)(2,1)S(1)}, bf16[4,4,4096]{2,1,0:T(4,128)(2,1)S(1)}, u32[]{:S(2)}, u32[]{:S(2)}) collective-permute-start(bf16[4,4,4096]{2,1,0:T(4,128)(2,1)S(1)} %get-tuple-element.35), channel_id=1, source_target_pairs={{0,32},{16,48},{32,0},{48,16},{1,33},{17,49},{33,1},{49,17},{2,34}... | collective-permute-start | bytes 393224 | tf_op jit(solution)/shard_map/ppermute | solution.py:177
  59.2 16.9 %collective-permute-start.11 = (bf16[4,4,4096]{2,1,0:T(4,128)(2,1)S(1)}, bf16[4,4,4096]{2,1,0:T(4,128)(2,1)S(1)}, u32[]{:S(2)}, u32[]{:S(2)}) collective-permute-start(bf16[4,4,4096]{2,1,0:T(4,128)(2,1)S(1)} %get-tuple-element.33), channel_id=1, source_target_pairs={{0,16},{16,32},{32,48},{48,0},{1,17},{17,33},{33,49},{49,1},{2,18}... | collective-permute-start | bytes 393224 | tf_op jit(solution)/shard_map/ppermute | solution.py:177
  70.8 15.4 %all-to-all-start.2 = ((bf16[8,32,1024]{2,1,0:T(8,128)(2,1)}), bf16[8,32,1024]{2,1,0:T(8,128)(2,1)S(1)}, u32[]{:S(2)}, u32[]{:S(2)}) async-start(bf16[8,32,1024]{2,1,0:T(8,128)(2,1)} %pad_maximum_fusion.1), calls=%async_computation.2 | async-start | bytes 1048576 | tf_op jit(solution)/shard_map/all_to_all | solution.py:193
  76.3 15.9 %collective-permute-start.16 = (f32[4,4096]{1,0:T(4,128)S(1)}, f32[4,4096]{1,0:T(4,128)S(1)}, u32[]{:S(2)}, u32[]{:S(2)}) collective-permute-start(f32[4,4096]{1,0:T(4,128)S(1)} %get-tuple-element.41), channel_id=1, source_target_pairs={{0,192},{64,0},{128,64},{192,128},{1,193},{65,1},{129,65},{193,129... | collective-permute-start | bytes 196616 | tf_op jit(solution)/shard_map/ppermute | solution.py:177
  77.4 14.8 %collective-permute-start.14 = (f32[4,4096]{1,0:T(4,128)S(1)}, f32[4,4096]{1,0:T(4,128)S(1)}, u32[]{:S(2)}, u32[]{:S(2)}) collective-permute-start(f32[4,4096]{1,0:T(4,128)S(1)} %get-tuple-element.42), channel_id=1, source_target_pairs={{0,64},{64,128},{128,192},{192,0},{1,65},{65,129},{129,193},{193,1... | collective-permute-start | bytes 196616 | tf_op jit(solution)/shard_map/ppermute | solution.py:177
  78.7 13.5 %collective-permute-start.15 = (f32[4,4096]{1,0:T(4,128)S(1)}, f32[4,4096]{1,0:T(4,128)S(1)}, u32[]{:S(2)}, u32[]{:S(2)}) collective-permute-start(f32[4,4096]{1,0:T(4,128)S(1)} %get-tuple-element.40), channel_id=1, source_target_pairs={{0,128},{64,192},{128,0},{192,64},{1,129},{65,193},{129,1},{193,65... | collective-permute-start | bytes 196616 | tf_op jit(solution)/shard_map/ppermute | solution.py:177
  87.1 18.0 %all-to-all-start.3 = ((bf16[32,32,128]{2,1,0:T(8,128)(2,1)}), bf16[32,32,128]{2,1,0:T(8,128)(2,1)S(1)}, u32[]{:S(2)}, u32[]{:S(2)}) async-start(bf16[32,32,128]{2,1,0:T(8,128)(2,1)} %broadcast_in_dim.26), calls=%async_computation.3 | async-start | bytes 524288 | tf_op jit(solution)/shard_map/all_to_all | solution.py:193

commit v2 on v1

--- a/solution.py
+++ b/solution.py
@@ -37,7 +37,7 @@
                 [jnp.where(first, u, v), jnp.where(first, v, u)], axis=0
             )
     b_ref[...] = rows[...].astype(BF)
-    b_copy = pltpu.make_async_copy(b_ref, b_out, sems.at[0])
+    b_copy = pltpu.make_async_copy(b_ref, b_out.at[pl.ds(0, S)], sems.at[0])
     b_copy.start()
     at[...] = a_ref[...].astype(F32).T.astype(BF)
     for n in range(C // 2):
@@ -50,7 +50,7 @@
                 x[d * C : (d + 1) * C, i * TJ : (i + 1) * TJ] = o[
                     i * C : (i + 1) * C, e * TJ : (e + 1) * TJ
                 ]
-    bias = bias_ref[...]
+    bias = bias_ref[0:1, :]
     total = jnp.zeros((8, CZ), F32)
     for q in range(8):
         pre_t = lax.dot_general(
@@ -63,7 +63,7 @@
         dpre = (g_ref[q * 512 : (q + 1) * 512, :].astype(F32) * slope).astype(BF)
         dp_ref[q * 512 : (q + 1) * 512, :] = dpre
         total = total + jnp.sum(dpre.astype(F32).reshape(64, 8, CZ), axis=0)
-    dp_copy = pltpu.make_async_copy(dp_ref, dp_out, sems.at[1])
+    dp_copy = pltpu.make_async_copy(dp_ref, dp_out.at[pl.ds(0, TI * TJ)], sems.at[1])
     dp_copy.start()
     po_copy = pltpu.make_async_copy(po_ref, po_out, sems.at[2])
     po_copy.start()
@@ -85,12 +85,19 @@
     pos_ref, dp_in, b_in, w_ref, a_ref, rm_ref, ro_ref, l_ref, dd, dp_ref, b_ref, sems
 ):
     first = pos_ref[2] == 0
-    dp_copy = pltpu.make_async_copy(dp_in, dp_ref, sems.at[0])
-    dp_copy.start()
-    b_copy = pltpu.make_async_copy(b_in, b_ref, sems.at[1])
+    dp_copies = [
+        pltpu.make_async_copy(
+            dp_in.at[pl.ds(1024 * n, 1024)], dp_ref.at[pl.ds(1024 * n, 1024)], sems.at[1 + n]
+        )
+        for n in range(4)
+    ]
+    for copy in dp_copies:
+        copy.start()
+    b_copy = pltpu.make_async_copy(b_in.at[pl.ds(0, S)], b_ref, sems.at[0])
     b_copy.start()
-    dp_copy.wait()
     for q in range(TI // 2):
+        if q % 4 == 0:
+            dp_copies[q // 4].wait()
         g = lax.dot_general(
             w_ref[...], dp_ref[q * 256 : (q + 1) * 256, :], NT, preferred_element_type=F32
         ).astype(BF)
@@ -131,8 +138,8 @@
         out_specs=(FAR, FAR, FAR, WHOLE),
         out_shape=(
             jax.ShapeDtypeStruct((TI * TJ, CZ), BF),
-            jax.ShapeDtypeStruct((TI * TJ, CZ), BF),
-            jax.ShapeDtypeStruct((S, C * TJ), BF),
+            jax.ShapeDtypeStruct((30 * TI * TJ, CZ), BF),
+            jax.ShapeDtypeStruct((30 * S, C * TJ), BF),
             jax.ShapeDtypeStruct((C, C + 8, CZ), BF),
         ),
         scratch_shapes=[
@@ -165,7 +172,7 @@
             pltpu.VMEM((TI * C, C * TJ), BF),
             pltpu.VMEM((TI * TJ, CZ), BF),
             pltpu.VMEM((S, C * TJ), BF),
-            pltpu.SemaphoreType.DMA((2,)),
+            pltpu.SemaphoreType.DMA((5,)),
         ],
         compiler_params=pltpu.CompilerParams(vmem_limit_bytes=40 << 20),
         cost_estimate=COST,
@@ -202,16 +209,17 @@
     mine = gather4(gather4(right_act.T.reshape(4, C * TJ), "h"), "x")
     left = (left_act * (1.0 / S)).astype(BF).reshape(TI, 16, C).transpose(1, 0, 2)
     a = spread(left.reshape(16, TI * C), COL, 8).reshape(S, TI * C)
-    mine, a = lax.optimization_barrier((mine, a))
+    bias = jnp.broadcast_to(out_bias, (8, CZ))
+    mine, a, bias = lax.optimization_barrier((mine, a, bias))
     other = swap(mine)
     w = out_weight.reshape(C, C, CZ).transpose(1, 0, 2).reshape(CC, CZ)
     pair_out, dp, b, wg = forward_call(
-        pos, a, mine, other, w.T, out_bias.reshape(1, CZ), pair_grad.reshape(TI * TJ, CZ)
+        pos, a, mine, other, w.T, bias, pair_grad.reshape(TI * TJ, CZ)
     )
     wg = exchange(wg, ROW)
     r_own, r_oth, l = backward_call(pos, dp, b, w, a)
     moved = [swap(r_oth[k]) for k in range(4)]
-    wg, l, _ = lax.optimization_barrier((wg, l, moved))
+    wg, l, r_own, moved = lax.optimization_barrier((wg, l, r_own, moved))
     wg = jnp.sum(wg.astype(F32), axis=0).reshape(5, TI * C)
     high = lax.reduce_precision(wg, 8, 7)
     pair = jnp.concatenate([high, wg - high, jnp.zeros((6, TI * C), F32)], axis=0).astype(BF)

time: 106 us -> 106 us (level)
  waiting for transfers between devices: 33.6 us -> 24.6 us
  starting transfers between devices: 46 us -> 50.9 us
  local copies, waits for them, and re-layouts: 6.3 us -> 8.46 us
    all_to_all x4, waiting for transfers between devices: 26.4 us -> 14 us  [exchange(): return lax.all_to_all(x, axes, split_axis=0, concat_axis=0, tiled=True)]
    all_to_all x4, starting transfers between devices: 19.5 us -> 25.4 us  [exchange(): return lax.all_to_all(x, axes, split_axis=0, concat_axis=0, tiled=True)]
    ppermute x12, waiting for transfers between devices: 6 us -> 9.12 us  [shift(): return lax.ppermute(x, axis, [(i, (i + k) % 4) for i in range(4)])]
    pallas_call x1, Pallas kernels: 7 us -> 8.41 us  [backward_call(): pl.pallas_call(backward_kernel, in_specs=[SCALARS, FAR, FAR, WHOLE, WHOLE...]
  transfers between devices with their start and end apart: 21 -> 21, of which waited for: 7 -> 11; matrix products, arithmetic and copies ran while one was open for 6% -> 8% of each run, Pallas kernels for 0% -> 8%
where the time goes in v2:
time: 106 us
  starting transfers between devices  50.9 us (48%)
  waiting for transfers between devices  24.6 us (23%)
  Pallas kernels  17 us (16%)
  local copies, waits for them, and re-layouts  8.46 us (8%)
  other arithmetic  3.84 us (4%)
    all_to_all x4, starting transfers between devices, exchange(): return lax.all_to_all(x, axes, split_axis=0, concat_axis=0, tiled=True)  25.4 us
    ppermute x12, starting transfers between devices, shift(): return lax.ppermute(x, axis, [(i, (i + k) % 4) for i in range(4)])  21.4 us
    all_to_all x4, waiting for transfers between devices, exchange(): return lax.all_to_all(x, axes, split_axis=0, concat_axis=0, tiled=True)  14 us
    ppermute x12, waiting for transfers between devices, shift(): return lax.ppermute(x, axis, [(i, (i + k) % 4) for i in range(4)])  9.12 us
    pallas_call x1, Pallas kernels, forward_call(): pl.pallas_call(forward_kernel, in_specs=[SCALARS] + [WHOLE] * 6, out_spec...  8.57 us
    pallas_call x1, Pallas kernels, backward_call(): pl.pallas_call(backward_kernel, in_specs=[SCALARS, FAR, FAR, WHOLE, WHOLE...  8.41 us
    ppermute x5, starting transfers between devices, swap(): return lax.ppermute(x, 'c', [(0, 1), (1, 0)])  4.15 us
  transfers between devices with their start and end apart: 21, of which 11 were waited for; matrix products, arithmetic and copies ran while one was open for 8% of the time, Pallas kernels for 8%

profile of v2, /device:TPU:1, one launch (start us, length us, event | category | flops | bytes accessed | tf_op | source)
XLA Modules:
  0.0 105.7 jit_solution(2576191413454711240)
XLA Ops:
  0.6 0.9 copy.21
  1.5 6.9 %collective-permute-start.2 = (bf16[4,4096]{1,0:T(4,128)(2,1)S(1)}, bf16[4,4096]{1,0:T(4,128)(2,1)S(1)}, u32[]{:S(2)}, u32[]{:S(2)}) collective-permute-start(bf16[4,4096]{1,0:T(4,128)(2,1)S(1)} %reshape.78), channel_id=1, source_target_pairs={{0,192},{64,0},{128,64},{192,128},{1,193},{65,1},{129,65},{193,129... | collective-permute-start | bytes 98312 | tf_op jit(solution)/shard_map/ppermute | solution.py:184
  8.5 1.0 collective-permute-start.1
  9.4 2.3 %collective-permute-start = (bf16[4,4096]{1,0:T(4,128)(2,1)S(1)}, bf16[4,4096]{1,0:T(4,128)(2,1)S(1)}, u32[]{:S(2)}, u32[]{:S(2)}) collective-permute-start(bf16[4,4096]{1,0:T(4,128)(2,1)S(1)} %reshape.78), channel_id=1, source_target_pairs={{0,64},{64,128},{128,192},{192,0},{1,65},{65,129},{129,193},{193,1... | collective-permute-start | bytes 98312 | tf_op jit(solution)/shard_map/ppermute | solution.py:184
  11.7 0.8 broadcast_multiply_fusion
  12.7 0.2 broadcast_in_dim.12
  12.8 0.7 broadcast_in_dim.26
  13.6 4.6 %all-to-all-start = ((bf16[8,16,1024]{2,1,0:T(8,128)(2,1)}), bf16[8,16,1024]{2,1,0:T(8,128)(2,1)S(1)}, u32[]{:S(2)}, u32[]{:S(2)}) async-start(bf16[8,16,1024]{2,1,0:T(8,128)(2,1)} %broadcast_in_dim.26), calls=%async_computation | async-start | bytes 524288 | tf_op jit(solution)/shard_map/all_to_all | solution.py:200
  18.4 2.6 %collective-permute-start.5 = (bf16[4,4,4096]{2,1,0:T(4,128)(2,1)S(1)}, bf16[4,4,4096]{2,1,0:T(4,128)(2,1)S(1)}, u32[]{:S(2)}, u32[]{:S(2)}) collective-permute-start(bf16[4,4,4096]{2,1,0:T(4,128)(2,1)S(1)} %pad_maximum_fusion.2), channel_id=1, source_target_pairs={{0,48},{16,0},{32,16},{48,32},{1,49},{17,1},{33,17},{49,33},{2,50}... | collective-permute-start | bytes 393224 | tf_op jit(solution)/shard_map/ppermute | solution.py:184
  20.9 0.5 collective-permute-start.4
  21.4 0.6 collective-permute-start.3
  22.2 1.2 %collective-permute-done.5 = bf16[4,4,4096]{2,1,0:T(4,128)(2,1)S(1)} collective-permute-done((bf16[4,4,4096]{2,1,0:T(4,128)(2,1)S(1)}, bf16[4,4,4096]{2,1,0:T(4,128)(2,1)S(1)}, u32[]{:S(2)}, u32[]{:S(2)}) %collective-permute-start.5) | collective-permute-done | bytes 131104 | tf_op jit(solution)/shard_map/ppermute | solution.py:184
  23.4 3.2 %collective-permute-done.4 = bf16[4,4,4096]{2,1,0:T(4,128)(2,1)S(1)} collective-permute-done((bf16[4,4,4096]{2,1,0:T(4,128)(2,1)S(1)}, bf16[4,4,4096]{2,1,0:T(4,128)(2,1)S(1)}, u32[]{:S(2)}, u32[]{:S(2)}) %collective-permute-start.4) | collective-permute-done | bytes 131104 | tf_op jit(solution)/shard_map/ppermute | solution.py:184
  26.5 1.6 %collective-permute-done.3 = bf16[4,4,4096]{2,1,0:T(4,128)(2,1)S(1)} collective-permute-done((bf16[4,4,4096]{2,1,0:T(4,128)(2,1)S(1)}, bf16[4,4,4096]{2,1,0:T(4,128)(2,1)S(1)}, u32[]{:S(2)}, u32[]{:S(2)}) %collective-permute-start.3) | collective-permute-done | bytes 131104 | tf_op jit(solution)/shard_map/ppermute | solution.py:184
  28.2 0.5 pad_maximum_fusion.mine_ref
  28.6 0.7 broadcast_in_dim.27.bias_ref
  29.3 3.0 %collective-permute-start.6 = (bf16[4,4,4,4096]{3,2,1,0:T(4,128)(2,1)S(1)}, bf16[4,4,4,4096]{3,2,1,0:T(4,128)(2,1)S(1)}, u32[]{:S(2)}, u32[]{:S(2)}) collective-permute-start(bf16[4,4,4,4096]{3,2,1,0:T(4,128)(2,1)S(1)} %pad_maximum_fusion.mine_ref), channel_id=1, source_target_pairs={{0,8},{8,0},{1,9},{9,1},{2,10},{10,2},{3,11},{11,3},{4,12},{12,4},... | collective-permute-start | bytes 1572872 | tf_op jit(solution)/shard_map/ppermute | solution.py:196
  32.3 1.1 copy.24
  33.6 0.2 collective-permute-done.6.other_ref
  33.8 1.2 %copy-done = bf16[32,128,128]{2,1,0:T(8,128)(2,1)S(1)} copy-done((bf16[32,128,128]{2,1,0:T(8,128)(2,1)S(1)}, bf16[32,128,128]{2,1,0:T(8,128)(2,1)}, u32[]{:S(2)}) %copy-start) | copy-done | bytes 1048600
  35.1 8.6 %forward.1 = (bf16[4096,128]{1,0:T(8,128)(2,1)}, bf16[122880,128]{1,0:T(8,128)(2,1)}, bf16[3840,4096]{1,0:T(8,128)(2,1)}, bf16[32,40,128]{2,1,0:T(8,128)(2,1)}) custom-call(s32[3]{0:T(128)S(1)} %pad_add_fusion.pos_ref, bf16[128,1024]{1,0:T(8,128)(2,1)S(1)} %bitcast.70, bf16[4,4,4,4096]{3,2,1,0:T(4,128)(2,1)S(1)} %pad_maximum_fusion.mine_ref, ...), custom_call_target="tpu_custom_call" | custom-call | flops 6442450944 | bytes 4194304 | tf_op jit(solution)/shard_map/forward/pallas_call | solution.py:135
  43.6 4.7 %all-to-all-start.1 = ((bf16[32,40,128]{2,1,0:T(8,128)(2,1)}), bf16[32,40,128]{2,1,0:T(8,128)(2,1)S(1)}, u32[]{:S(2)}, u32[]{:S(2)}) async-start(bf16[32,40,128]{2,1,0:T(8,128)(2,1)} %get-tuple-element.29), calls=%async_computation.1 | async-start | bytes 655360 | tf_op jit(solution)/shard_map/all_to_all | solution.py:200
  48.4 8.4 %backward.1 = (f32[4,4,4,4096]{3,2,1,0:T(4,128)S(1)}, bf16[4,4,4,4096]{3,2,1,0:T(4,128)(2,1)S(1)}, bf16[128,1024]{1,0:T(8,128)(2,1)S(1)}) custom-call(s32[3]{0:T(128)S(1)} %pad_add_fusion.pos_ref, bf16[122880,128]{1,0:T(8,128)(2,1)} %get-tuple-element.30.dp_in, bf16[3840,4096]{1,0:T(8,128)(2,1)} %get-tuple-element.31.b_in, bf16[1024,128]{1,0:T(8,128)(2,1)S(1)} %bitcast.69, ...), custom_call_target="tpu_custom_call" | custom-call | flops 6442450944 | bytes 4194304 | tf_op jit(solution)/shard_map/backward/pallas_call | solution.py:162
  56.8 0.2 slice_bitcast_fusion
  57.0 0.5 collective-permute-start.7
  57.7 0.4 collective-permute-start.9
  58.2 0.3 collective-permute-done.7
  58.5 0.4 collective-permute-done.8
  58.9 0.2 collective-permute-done.9
  59.1 0.3 collective-permute-done.10
  59.4 3.3 %all-to-all-done.1 = bf16[32,40,128]{2,1,0:T(8,128)(2,1)S(1)} async-done(((bf16[32,40,128]{2,1,0:T(8,128)(2,1)}), bf16[32,40,128]{2,1,0:T(8,128)(2,1)S(1)}, u32[]{:S(2)}, u32[]{:S(2)}) %all-to-all-start.1) | async-done | bytes 327712 | tf_op jit(solution)/shard_map/all_to_all | solution.py:200
  62.8 0.2 fusion.2
  63.0 2.0 %collective-permute-start.13 = (bf16[4,4,4096]{2,1,0:T(4,128)(2,1)S(1)}, bf16[4,4,4096]{2,1,0:T(4,128)(2,1)S(1)}, u32[]{:S(2)}, u32[]{:S(2)}) collective-permute-start(bf16[4,4,4096]{2,1,0:T(4,128)(2,1)S(1)} %get-tuple-element.46), channel_id=1, source_target_pairs={{0,48},{16,0},{32,16},{48,32},{1,49},{17,1},{33,17},{49,33},{2,50}... | collective-permute-start | bytes 393224 | tf_op jit(solution)/shard_map/ppermute | solution.py:184
  65.1 0.4 collective-permute-start.12
  65.5 0.3 collective-permute-start.11
  65.9 0.8 pad_maximum_fusion.1
  66.7 5.0 %all-to-all-start.2 = ((bf16[8,32,1024]{2,1,0:T(8,128)(2,1)}), bf16[8,32,1024]{2,1,0:T(8,128)(2,1)S(1)}, u32[]{:S(2)}, u32[]{:S(2)}) async-start(bf16[8,32,1024]{2,1,0:T(8,128)(2,1)} %pad_maximum_fusion.1), calls=%async_computation.2 | async-start | bytes 1048576 | tf_op jit(solution)/shard_map/all_to_all | solution.py:200
  71.7 3.1 %collective-permute-done.11 = bf16[4,4,4096]{2,1,0:T(4,128)(2,1)S(1)} collective-permute-done((bf16[4,4,4096]{2,1,0:T(4,128)(2,1)S(1)}, bf16[4,4,4096]{2,1,0:T(4,128)(2,1)S(1)}, u32[]{:S(2)}, u32[]{:S(2)}) %collective-permute-start.11) | collective-permute-done | bytes 131104 | tf_op jit(solution)/shard_map/ppermute | solution.py:184
  75.0 0.7 collective-permute-start.16
  75.7 1.8 %collective-permute-start.14 = (f32[4,4096]{1,0:T(4,128)S(1)}, f32[4,4096]{1,0:T(4,128)S(1)}, u32[]{:S(2)}, u32[]{:S(2)}) collective-permute-start(f32[4,4096]{1,0:T(4,128)S(1)} %get-tuple-element.54), channel_id=1, source_target_pairs={{0,64},{64,128},{128,192},{192,0},{1,65},{65,129},{129,193},{193,1... | collective-permute-start | bytes 196616 | tf_op jit(solution)/shard_map/ppermute | solution.py:184
  77.4 2.3 %collective-permute-start.15 = (f32[4,4096]{1,0:T(4,128)S(1)}, f32[4,4096]{1,0:T(4,128)S(1)}, u32[]{:S(2)}, u32[]{:S(2)}) collective-permute-start(f32[4,4096]{1,0:T(4,128)S(1)} %get-tuple-element.52), channel_id=1, source_target_pairs={{0,128},{64,192},{128,0},{192,64},{1,129},{65,193},{129,1},{193,65... | collective-permute-start | bytes 196616 | tf_op jit(solution)/shard_map/ppermute | solution.py:184
  79.9 0.7 broadcast_in_dim.30
  80.6 11.1 %all-to-all-start.3 = ((bf16[32,32,128]{2,1,0:T(8,128)(2,1)}), bf16[32,32,128]{2,1,0:T(8,128)(2,1)S(1)}, u32[]{:S(2)}, u32[]{:S(2)}) async-start(bf16[32,32,128]{2,1,0:T(8,128)(2,1)} %broadcast_in_dim.30), calls=%async_computation.3 | async-start | bytes 524288 | tf_op jit(solution)/shard_map/all_to_all | solution.py:200
  91.8 0.7 copy.27
  92.9 0.8 reshape.88
  93.6 0.5 slice_bitcast_fusion.8
  94.2 10.7 %all-to-all-done.3 = bf16[32,32,128]{2,1,0:T(8,128)(2,1)S(1)} async-done(((bf16[32,32,128]{2,1,0:T(8,128)(2,1)}), bf16[32,32,128]{2,1,0:T(8,128)(2,1)S(1)}, u32[]{:S(2)}, u32[]{:S(2)}) %all-to-all-start.3) | async-done | bytes 262176 | tf_op jit(solution)/shard_map/all_to_all | solution.py:200
  104.9 0.8 bitcast_convert_fusion
  (40 shorter events, 1.8 us)
Async XLA Ops:
  1.5 16.7 %collective-permute-start.2 = (bf16[4,4096]{1,0:T(4,128)(2,1)S(1)}, bf16[4,4096]{1,0:T(4,128)(2,1)S(1)}, u32[]{:S(2)}, u32[]{:S(2)}) collective-permute-start(bf16[4,4096]{1,0:T(4,128)(2,1)S(1)} %reshape.78), channel_id=1, source_target_pairs={{0,192},{64,0},{128,64},{192,128},{1,193},{65,1},{129,65},{193,129... | collective-permute-start | bytes 98312 | tf_op jit(solution)/shard_map/ppermute | solution.py:184
  8.5 9.8 %collective-permute-start.1 = (bf16[4,4096]{1,0:T(4,128)(2,1)S(1)}, bf16[4,4096]{1,0:T(4,128)(2,1)S(1)}, u32[]{:S(2)}, u32[]{:S(2)}) collective-permute-start(bf16[4,4096]{1,0:T(4,128)(2,1)S(1)} %reshape.78), channel_id=1, source_target_pairs={{0,128},{64,192},{128,0},{192,64},{1,129},{65,193},{129,1},{193,65... | collective-permute-start | bytes 98312 | tf_op jit(solution)/shard_map/ppermute | solution.py:184
  9.4 8.8 %collective-permute-start = (bf16[4,4096]{1,0:T(4,128)(2,1)S(1)}, bf16[4,4096]{1,0:T(4,128)(2,1)S(1)}, u32[]{:S(2)}, u32[]{:S(2)}) collective-permute-start(bf16[4,4096]{1,0:T(4,128)(2,1)S(1)} %reshape.78), channel_id=1, source_target_pairs={{0,64},{64,128},{128,192},{192,0},{1,65},{65,129},{129,193},{193,1... | collective-permute-start | bytes 98312 | tf_op jit(solution)/shard_map/ppermute | solution.py:184
  13.6 15.1 %all-to-all-start = ((bf16[8,16,1024]{2,1,0:T(8,128)(2,1)}), bf16[8,16,1024]{2,1,0:T(8,128)(2,1)S(1)}, u32[]{:S(2)}, u32[]{:S(2)}) async-start(bf16[8,16,1024]{2,1,0:T(8,128)(2,1)} %broadcast_in_dim.26), calls=%async_computation | async-start | bytes 524288 | tf_op jit(solution)/shard_map/all_to_all | solution.py:200
  18.4 5.0 %collective-permute-start.5 = (bf16[4,4,4096]{2,1,0:T(4,128)(2,1)S(1)}, bf16[4,4,4096]{2,1,0:T(4,128)(2,1)S(1)}, u32[]{:S(2)}, u32[]{:S(2)}) collective-permute-start(bf16[4,4,4096]{2,1,0:T(4,128)(2,1)S(1)} %pad_maximum_fusion.2), channel_id=1, source_target_pairs={{0,48},{16,0},{32,16},{48,32},{1,49},{17,1},{33,17},{49,33},{2,50}... | collective-permute-start | bytes 393224 | tf_op jit(solution)/shard_map/ppermute | solution.py:184
  20.9 5.6 %collective-permute-start.4 = (bf16[4,4,4096]{2,1,0:T(4,128)(2,1)S(1)}, bf16[4,4,4096]{2,1,0:T(4,128)(2,1)S(1)}, u32[]{:S(2)}, u32[]{:S(2)}) collective-permute-start(bf16[4,4,4096]{2,1,0:T(4,128)(2,1)S(1)} %pad_maximum_fusion.2), channel_id=1, source_target_pairs={{0,32},{16,48},{32,0},{48,16},{1,33},{17,49},{33,1},{49,17},{2,34}... | collective-permute-start | bytes 393224 | tf_op jit(solution)/shard_map/ppermute | solution.py:184
  21.4 6.7 %collective-permute-start.3 = (bf16[4,4,4096]{2,1,0:T(4,128)(2,1)S(1)}, bf16[4,4,4096]{2,1,0:T(4,128)(2,1)S(1)}, u32[]{:S(2)}, u32[]{:S(2)}) collective-permute-start(bf16[4,4,4096]{2,1,0:T(4,128)(2,1)S(1)} %pad_maximum_fusion.2), channel_id=1, source_target_pairs={{0,16},{16,32},{32,48},{48,0},{1,17},{17,33},{33,49},{49,1},{2,18}... | collective-permute-start | bytes 393224 | tf_op jit(solution)/shard_map/ppermute | solution.py:184
  29.3 4.5 %collective-permute-start.6 = (bf16[4,4,4,4096]{3,2,1,0:T(4,128)(2,1)S(1)}, bf16[4,4,4,4096]{3,2,1,0:T(4,128)(2,1)S(1)}, u32[]{:S(2)}, u32[]{:S(2)}) collective-permute-start(bf16[4,4,4,4096]{3,2,1,0:T(4,128)(2,1)S(1)} %pad_maximum_fusion.mine_ref), channel_id=1, source_target_pairs={{0,8},{8,0},{1,9},{9,1},{2,10},{10,2},{3,11},{11,3},{4,12},{12,4},... | collective-permute-start | bytes 1572872 | tf_op jit(solution)/shard_map/ppermute | solution.py:196
  33.8 1.2 %copy-start = (bf16[32,128,128]{2,1,0:T(8,128)(2,1)S(1)}, bf16[32,128,128]{2,1,0:T(8,128)(2,1)}, u32[]{:S(2)}) copy-start(bf16[32,128,128]{2,1,0:T(8,128)(2,1)} %param.9) | copy-start | bytes 3145732
  43.6 19.1 %all-to-all-start.1 = ((bf16[32,40,128]{2,1,0:T(8,128)(2,1)}), bf16[32,40,128]{2,1,0:T(8,128)(2,1)S(1)}, u32[]{:S(2)}, u32[]{:S(2)}) async-start(bf16[32,40,128]{2,1,0:T(8,128)(2,1)} %get-tuple-element.29), calls=%async_computation.1 | async-start | bytes 655360 | tf_op jit(solution)/shard_map/all_to_all | solution.py:200
  57.0 1.5 %collective-permute-start.7 = (bf16[4,4,4096]{2,1,0:T(4,128)(2,1)S(1)}, bf16[4,4,4096]{2,1,0:T(4,128)(2,1)S(1)}, u32[]{:S(2)}, u32[]{:S(2)}) collective-permute-start(bf16[4,4,4096]{2,1,0:T(4,128)(2,1)S(1)} %get-tuple-element.51), channel_id=1, source_target_pairs={{0,8},{8,0},{1,9},{9,1},{2,10},{10,2},{3,11},{11,3},{4,12},{12,4},... | collective-permute-start | bytes 393224 | tf_op jit(solution)/shard_map/ppermute | solution.py:196
  57.6 1.3 %collective-permute-start.8 = (bf16[4,4,4096]{2,1,0:T(4,128)(2,1)S(1)}, bf16[4,4,4096]{2,1,0:T(4,128)(2,1)S(1)}, u32[]{:S(2)}, u32[]{:S(2)}) collective-permute-start(bf16[4,4,4096]{2,1,0:T(4,128)(2,1)S(1)} %get-tuple-element.50), channel_id=1, source_target_pairs={{0,8},{8,0},{1,9},{9,1},{2,10},{10,2},{3,11},{11,3},{4,12},{12,4},... | collective-permute-start | bytes 393224 | tf_op jit(solution)/shard_map/ppermute | solution.py:196
  57.7 1.4 %collective-permute-start.9 = (bf16[4,4,4096]{2,1,0:T(4,128)(2,1)S(1)}, bf16[4,4,4096]{2,1,0:T(4,128)(2,1)S(1)}, u32[]{:S(2)}, u32[]{:S(2)}) collective-permute-start(bf16[4,4,4096]{2,1,0:T(4,128)(2,1)S(1)} %get-tuple-element.49), channel_id=1, source_target_pairs={{0,8},{8,0},{1,9},{9,1},{2,10},{10,2},{3,11},{11,3},{4,12},{12,4},... | collective-permute-start | bytes 393224 | tf_op jit(solution)/shard_map/ppermute | solution.py:196
  58.1 1.3 %collective-permute-start.10 = (bf16[4,4,4096]{2,1,0:T(4,128)(2,1)S(1)}, bf16[4,4,4096]{2,1,0:T(4,128)(2,1)S(1)}, u32[]{:S(2)}, u32[]{:S(2)}) collective-permute-start(bf16[4,4,4096]{2,1,0:T(4,128)(2,1)S(1)} %get-tuple-element.48), channel_id=1, source_target_pairs={{0,8},{8,0},{1,9},{9,1},{2,10},{10,2},{3,11},{11,3},{4,12},{12,4},... | collective-permute-start | bytes 393224 | tf_op jit(solution)/shard_map/ppermute | solution.py:196
  63.0 8.6 %collective-permute-start.13 = (bf16[4,4,4096]{2,1,0:T(4,128)(2,1)S(1)}, bf16[4,4,4096]{2,1,0:T(4,128)(2,1)S(1)}, u32[]{:S(2)}, u32[]{:S(2)}) collective-permute-start(bf16[4,4,4096]{2,1,0:T(4,128)(2,1)S(1)} %get-tuple-element.46), channel_id=1, source_target_pairs={{0,48},{16,0},{32,16},{48,32},{1,49},{17,1},{33,17},{49,33},{2,50}... | collective-permute-start | bytes 393224 | tf_op jit(solution)/shard_map/ppermute | solution.py:184
  65.1 6.6 %collective-permute-start.12 = (bf16[4,4,4096]{2,1,0:T(4,128)(2,1)S(1)}, bf16[4,4,4096]{2,1,0:T(4,128)(2,1)S(1)}, u32[]{:S(2)}, u32[]{:S(2)}) collective-permute-start(bf16[4,4,4096]{2,1,0:T(4,128)(2,1)S(1)} %get-tuple-element.47), channel_id=1, source_target_pairs={{0,32},{16,48},{32,0},{48,16},{1,33},{17,49},{33,1},{49,17},{2,34}... | collective-permute-start | bytes 393224 | tf_op jit(solution)/shard_map/ppermute | solution.py:184
  65.5 9.3 %collective-permute-start.11 = (bf16[4,4,4096]{2,1,0:T(4,128)(2,1)S(1)}, bf16[4,4,4096]{2,1,0:T(4,128)(2,1)S(1)}, u32[]{:S(2)}, u32[]{:S(2)}) collective-permute-start(bf16[4,4,4096]{2,1,0:T(4,128)(2,1)S(1)} %get-tuple-element.45), channel_id=1, source_target_pairs={{0,16},{16,32},{32,48},{48,0},{1,17},{17,33},{33,49},{49,1},{2,18}... | collective-permute-start | bytes 393224 | tf_op jit(solution)/shard_map/ppermute | solution.py:184
  66.7 13.1 %all-to-all-start.2 = ((bf16[8,32,1024]{2,1,0:T(8,128)(2,1)}), bf16[8,32,1024]{2,1,0:T(8,128)(2,1)S(1)}, u32[]{:S(2)}, u32[]{:S(2)}) async-start(bf16[8,32,1024]{2,1,0:T(8,128)(2,1)} %pad_maximum_fusion.1), calls=%async_computation.2 | async-start | bytes 1048576 | tf_op jit(solution)/shard_map/all_to_all | solution.py:200
  75.0 16.7 %collective-permute-start.16 = (f32[4,4096]{1,0:T(4,128)S(1)}, f32[4,4096]{1,0:T(4,128)S(1)}, u32[]{:S(2)}, u32[]{:S(2)}) collective-permute-start(f32[4,4096]{1,0:T(4,128)S(1)} %get-tuple-element.53), channel_id=1, source_target_pairs={{0,192},{64,0},{128,64},{192,128},{1,193},{65,1},{129,65},{193,129... | collective-permute-start | bytes 196616 | tf_op jit(solution)/shard_map/ppermute | solution.py:184
  75.7 16.1 %collective-permute-start.14 = (f32[4,4096]{1,0:T(4,128)S(1)}, f32[4,4096]{1,0:T(4,128)S(1)}, u32[]{:S(2)}, u32[]{:S(2)}) collective-permute-start(f32[4,4096]{1,0:T(4,128)S(1)} %get-tuple-element.54), channel_id=1, source_target_pairs={{0,64},{64,128},{128,192},{192,0},{1,65},{65,129},{129,193},{193,1... | collective-permute-start | bytes 196616 | tf_op jit(solution)/shard_map/ppermute | solution.py:184
  77.4 14.3 %collective-permute-start.15 = (f32[4,4096]{1,0:T(4,128)S(1)}, f32[4,4096]{1,0:T(4,128)S(1)}, u32[]{:S(2)}, u32[]{:S(2)}) collective-permute-start(f32[4,4096]{1,0:T(4,128)S(1)} %get-tuple-element.52), channel_id=1, source_target_pairs={{0,128},{64,192},{128,0},{192,64},{1,129},{65,193},{129,1},{193,65... | collective-permute-start | bytes 196616 | tf_op jit(solution)/shard_map/ppermute | solution.py:184
  80.6 24.2 %all-to-all-start.3 = ((bf16[32,32,128]{2,1,0:T(8,128)(2,1)}), bf16[32,32,128]{2,1,0:T(8,128)(2,1)S(1)}, u32[]{:S(2)}, u32[]{:S(2)}) async-start(bf16[32,32,128]{2,1,0:T(8,128)(2,1)} %broadcast_in_dim.30), calls=%async_computation.3 | async-start | bytes 524288 | tf_op jit(solution)/shard_map/all_to_all | solution.py:200

commit v3 on v2

--- a/solution.py
+++ b/solution.py
@@ -221,17 +221,19 @@
     moved = [swap(r_oth[k]) for k in range(4)]
     wg, l, r_own, moved = lax.optimization_barrier((wg, l, r_own, moved))
     wg = jnp.sum(wg.astype(F32), axis=0).reshape(5, TI * C)
-    high = lax.reduce_precision(wg, 8, 7)
-    pair = jnp.concatenate([high, wg - high, jnp.zeros((6, TI * C), F32)], axis=0).astype(BF)
     both = exchange(
         jnp.concatenate(
-            [l.reshape(8, 16, TI * C), jnp.broadcast_to(pair[None], (8, 16, TI * C))], axis=1
+            [
+                l.reshape(8, 16, TI * C),
+                jnp.broadcast_to(jnp.pad(wg.astype(BF), ((0, 3), (0, 0)))[None], (8, 8, TI * C)),
+            ],
+            axis=1,
         ),
         COL,
     )
     both = jnp.sum(both.astype(F32), axis=0)
     left_grad = both[:16].reshape(16, TI, C).transpose(1, 0, 2).reshape(TI, 16 * C)
-    wg = (both[16:21] + both[21:26]).reshape(C + 8, CZ) * (1.0 / (TI * 32))
+    wg = both[16:21].reshape(C + 8, CZ) * (1.0 / (TI * 32))
     bias_grad = wg[C]
     full = spread(wg[:C].astype(BF), ROW, 32)
     full, left_grad, bias_grad = lax.optimization_barrier((full, left_grad, bias_grad))

time: 106 us -> 106 us (level)
  waiting for transfers between devices: 24.6 us -> 20.3 us
  starting transfers between devices: 50.9 us -> 54.8 us
    ppermute x12, waiting for transfers between devices: 9.12 us -> 4.21 us  [shift(): return lax.ppermute(x, axis, [(i, (i + k) % 4) for i in range(4)])]
    ppermute x12, starting transfers between devices: 21.4 us -> 24.2 us  [shift(): return lax.ppermute(x, axis, [(i, (i + k) % 4) for i in range(4)])]
    all_to_all x4, starting transfers between devices: 25.4 us -> 27.7 us  [exchange(): return lax.all_to_all(x, axes, split_axis=0, concat_axis=0, tiled=True)]
    ppermute x5, starting transfers between devices: 4.15 us -> 2.88 us  [swap(): return lax.ppermute(x, 'c', [(0, 1), (1, 0)])]
  transfers between devices with their start and end apart: 21 -> 21, of which waited for: 11 -> 10; matrix products, arithmetic and copies ran while one was open for 8% -> 8% of each run, Pallas kernels for 8% -> 8%
where the time goes in v3:
time: 106 us; the launch traced here: 105 us
  starting transfers between devices  54.8 us (52%)
  waiting for transfers between devices  20.3 us (19%)
  Pallas kernels  17 us (16%)
  local copies, waits for them, and re-layouts  8.41 us (8%)
  other arithmetic  3.68 us (3%)
    all_to_all x4, starting transfers between devices, exchange(): return lax.all_to_all(x, axes, split_axis=0, concat_axis=0, tiled=True)  27.7 us
    ppermute x12, starting transfers between devices, shift(): return lax.ppermute(x, axis, [(i, (i + k) % 4) for i in range(4)])  24.2 us
    all_to_all x4, waiting for transfers between devices, exchange(): return lax.all_to_all(x, axes, split_axis=0, concat_axis=0, tiled=True)  14.6 us
    pallas_call x1, Pallas kernels, forward_call(): pl.pallas_call(forward_kernel, in_specs=[SCALARS] + [WHOLE] * 6, out_spec...  8.57 us
    pallas_call x1, Pallas kernels, backward_call(): pl.pallas_call(backward_kernel, in_specs=[SCALARS, FAR, FAR, WHOLE, WHOLE...  8.41 us
    ppermute x12, waiting for transfers between devices, shift(): return lax.ppermute(x, axis, [(i, (i + k) % 4) for i in range(4)])  4.21 us
    ppermute x5, starting transfers between devices, swap(): return lax.ppermute(x, 'c', [(0, 1), (1, 0)])  2.88 us
  transfers between devices with their start and end apart: 21, of which 10 were waited for; matrix products, arithmetic and copies ran while one was open for 8% of the time, Pallas kernels for 8%

profile of v3, /device:TPU:1, one launch (start us, length us, event | category | flops | bytes accessed | tf_op | source)
XLA Modules:
  0.0 105.1 jit_solution(3040836348594262530)
XLA Ops:
  0.6 0.9 copy.21
  1.5 6.9 %collective-permute-start.2 = (bf16[4,4096]{1,0:T(4,128)(2,1)S(1)}, bf16[4,4096]{1,0:T(4,128)(2,1)S(1)}, u32[]{:S(2)}, u32[]{:S(2)}) collective-permute-start(bf16[4,4096]{1,0:T(4,128)(2,1)S(1)} %reshape.59), channel_id=1, source_target_pairs={{0,192},{64,0},{128,64},{192,128},{1,193},{65,1},{129,65},{193,129... | collective-permute-start | bytes 98312 | tf_op jit(solution)/shard_map/ppermute | solution.py:184
  8.5 1.0 collective-permute-start.1
  9.4 2.3 %collective-permute-start = (bf16[4,4096]{1,0:T(4,128)(2,1)S(1)}, bf16[4,4096]{1,0:T(4,128)(2,1)S(1)}, u32[]{:S(2)}, u32[]{:S(2)}) collective-permute-start(bf16[4,4096]{1,0:T(4,128)(2,1)S(1)} %reshape.59), channel_id=1, source_target_pairs={{0,64},{64,128},{128,192},{192,0},{1,65},{65,129},{129,193},{193,1... | collective-permute-start | bytes 98312 | tf_op jit(solution)/shard_map/ppermute | solution.py:184
  11.7 0.8 broadcast_multiply_fusion
  12.7 0.2 broadcast_in_dim.10
  12.8 0.7 broadcast_in_dim.11
  13.6 4.6 %all-to-all-start = ((bf16[8,16,1024]{2,1,0:T(8,128)(2,1)}), bf16[8,16,1024]{2,1,0:T(8,128)(2,1)S(1)}, u32[]{:S(2)}, u32[]{:S(2)}) async-start(bf16[8,16,1024]{2,1,0:T(8,128)(2,1)} %broadcast_in_dim.11), calls=%async_computation | async-start | bytes 524288 | tf_op jit(solution)/shard_map/all_to_all | solution.py:200
  18.4 2.8 %collective-permute-start.4 = (bf16[4,4,4096]{2,1,0:T(4,128)(2,1)S(1)}, bf16[4,4,4096]{2,1,0:T(4,128)(2,1)S(1)}, u32[]{:S(2)}, u32[]{:S(2)}) collective-permute-start(bf16[4,4,4096]{2,1,0:T(4,128)(2,1)S(1)} %pad_maximum_fusion.2), channel_id=1, source_target_pairs={{0,32},{16,48},{32,0},{48,16},{1,33},{17,49},{33,1},{49,17},{2,34}... | collective-permute-start | bytes 393224 | tf_op jit(solution)/shard_map/ppermute | solution.py:184
  21.2 0.3 collective-permute-start.3
  21.5 2.4 %collective-permute-start.5 = (bf16[4,4,4096]{2,1,0:T(4,128)(2,1)S(1)}, bf16[4,4,4096]{2,1,0:T(4,128)(2,1)S(1)}, u32[]{:S(2)}, u32[]{:S(2)}) collective-permute-start(bf16[4,4,4096]{2,1,0:T(4,128)(2,1)S(1)} %pad_maximum_fusion.2), channel_id=1, source_target_pairs={{0,48},{16,0},{32,16},{48,32},{1,49},{17,1},{33,17},{49,33},{2,50}... | collective-permute-start | bytes 393224 | tf_op jit(solution)/shard_map/ppermute | solution.py:184
  24.0 3.9 %collective-permute-done.3 = bf16[4,4,4096]{2,1,0:T(4,128)(2,1)S(1)} collective-permute-done((bf16[4,4,4096]{2,1,0:T(4,128)(2,1)S(1)}, bf16[4,4,4096]{2,1,0:T(4,128)(2,1)S(1)}, u32[]{:S(2)}, u32[]{:S(2)}) %collective-permute-start.3) | collective-permute-done | bytes 131104 | tf_op jit(solution)/shard_map/ppermute | solution.py:184
  27.9 0.5 pad_maximum_fusion.mine_ref
  28.3 0.7 broadcast_in_dim.24.bias_ref
  29.0 1.7 %collective-permute-start.6 = (bf16[4,4,4,4096]{3,2,1,0:T(4,128)(2,1)S(1)}, bf16[4,4,4,4096]{3,2,1,0:T(4,128)(2,1)S(1)}, u32[]{:S(2)}, u32[]{:S(2)}) collective-permute-start(bf16[4,4,4,4096]{3,2,1,0:T(4,128)(2,1)S(1)} %pad_maximum_fusion.mine_ref), channel_id=1, source_target_pairs={{0,8},{8,0},{1,9},{9,1},{2,10},{10,2},{3,11},{11,3},{4,12},{12,4},... | collective-permute-start | bytes 1572872 | tf_op jit(solution)/shard_map/ppermute | solution.py:196
  30.7 1.1 %copy.24 = bf16[32,32,128]{2,0,1:T(8,128)(2,1)S(1)} copy(bf16[32,32,128]{2,1,0:T(8,128)(2,1)} %bitcast.76) | data formatting | bytes 524288 | tf_op jit(solution)/shard_map/reshape | solution.py:215
  32.0 0.2 collective-permute-done.6.other_ref
  32.3 1.2 %copy-done = bf16[32,128,128]{2,1,0:T(8,128)(2,1)S(1)} copy-done((bf16[32,128,128]{2,1,0:T(8,128)(2,1)S(1)}, bf16[32,128,128]{2,1,0:T(8,128)(2,1)}, u32[]{:S(2)}) %copy-start) | copy-done | bytes 1048600
  33.5 8.6 %forward.1 = (bf16[4096,128]{1,0:T(8,128)(2,1)}, bf16[122880,128]{1,0:T(8,128)(2,1)}, bf16[3840,4096]{1,0:T(8,128)(2,1)}, bf16[32,40,128]{2,1,0:T(8,128)(2,1)}) custom-call(s32[3]{0:T(128)S(1)} %pad_add_fusion.pos_ref, bf16[128,1024]{1,0:T(8,128)(2,1)S(1)} %bitcast.70, bf16[4,4,4,4096]{3,2,1,0:T(4,128)(2,1)S(1)} %pad_maximum_fusion.mine_ref, ...), custom_call_target="tpu_custom_call" | custom-call | flops 6442450944 | bytes 4194304 | tf_op jit(solution)/shard_map/forward/pallas_call | solution.py:135
  42.1 7.0 %all-to-all-start.1 = ((bf16[32,40,128]{2,1,0:T(8,128)(2,1)}), bf16[32,40,128]{2,1,0:T(8,128)(2,1)S(1)}, u32[]{:S(2)}, u32[]{:S(2)}) async-start(bf16[32,40,128]{2,1,0:T(8,128)(2,1)} %get-tuple-element.29), calls=%async_computation.1 | async-start | bytes 655360 | tf_op jit(solution)/shard_map/all_to_all | solution.py:200
  49.1 8.4 %backward.1 = (f32[4,4,4,4096]{3,2,1,0:T(4,128)S(1)}, bf16[4,4,4,4096]{3,2,1,0:T(4,128)(2,1)S(1)}, bf16[128,1024]{1,0:T(8,128)(2,1)S(1)}) custom-call(s32[3]{0:T(128)S(1)} %pad_add_fusion.pos_ref, bf16[122880,128]{1,0:T(8,128)(2,1)} %get-tuple-element.30.dp_in, bf16[3840,4096]{1,0:T(8,128)(2,1)} %get-tuple-element.31.b_in, bf16[1024,128]{1,0:T(8,128)(2,1)S(1)} %bitcast.69, ...), custom_call_target="tpu_custom_call" | custom-call | flops 6442450944 | bytes 4194304 | tf_op jit(solution)/shard_map/backward/pallas_call | solution.py:162
  57.6 0.2 slice_bitcast_fusion
  57.7 0.5 collective-permute-start.10
  58.4 0.4 collective-permute-start.8
  58.9 0.4 collective-permute-done.10
  59.3 0.4 collective-permute-done.9
  59.6 0.2 collective-permute-done.8
  59.8 0.3 collective-permute-done.7
  60.1 3.3 %all-to-all-done.1 = bf16[32,40,128]{2,1,0:T(8,128)(2,1)S(1)} async-done(((bf16[32,40,128]{2,1,0:T(8,128)(2,1)}), bf16[32,40,128]{2,1,0:T(8,128)(2,1)S(1)}, u32[]{:S(2)}, u32[]{:S(2)}) %all-to-all-start.1) | async-done | bytes 327712 | tf_op jit(solution)/shard_map/all_to_all | solution.py:200
  63.5 0.2 fusion.2
  63.7 0.7 collective-permute-start.11
  64.4 2.1 %collective-permute-start.13 = (bf16[4,4,4096]{2,1,0:T(4,128)(2,1)S(1)}, bf16[4,4,4096]{2,1,0:T(4,128)(2,1)S(1)}, u32[]{:S(2)}, u32[]{:S(2)}) collective-permute-start(bf16[4,4,4096]{2,1,0:T(4,128)(2,1)S(1)} %get-tuple-element.46), channel_id=1, source_target_pairs={{0,48},{16,0},{32,16},{48,32},{1,49},{17,1},{33,17},{49,33},{2,50}... | collective-permute-start | bytes 393224 | tf_op jit(solution)/shard_map/ppermute | solution.py:184
  66.4 0.5 collective-permute-start.12
  67.1 0.8 pad_maximum_fusion.1
  67.8 5.2 %all-to-all-start.2 = ((bf16[8,24,1024]{2,1,0:T(8,128)(2,1)}), bf16[8,24,1024]{2,1,0:T(8,128)(2,1)S(1)}, u32[]{:S(2)}, u32[]{:S(2)}) async-start(bf16[8,24,1024]{2,1,0:T(8,128)(2,1)} %pad_maximum_fusion.1), calls=%async_computation.2 | async-start | bytes 786432 | tf_op jit(solution)/shard_map/all_to_all | solution.py:200
  73.1 0.3 collective-permute-done.12
  73.6 2.9 %collective-permute-start.15 = (f32[4,4096]{1,0:T(4,128)S(1)}, f32[4,4096]{1,0:T(4,128)S(1)}, u32[]{:S(2)}, u32[]{:S(2)}) collective-permute-start(f32[4,4096]{1,0:T(4,128)S(1)} %get-tuple-element.52), channel_id=1, source_target_pairs={{0,128},{64,192},{128,0},{192,64},{1,129},{65,193},{129,1},{193,65... | collective-permute-start | bytes 196616 | tf_op jit(solution)/shard_map/ppermute | solution.py:184
  76.5 0.7 collective-permute-start.16
  77.2 1.7 %collective-permute-start.14 = (f32[4,4096]{1,0:T(4,128)S(1)}, f32[4,4096]{1,0:T(4,128)S(1)}, u32[]{:S(2)}, u32[]{:S(2)}) collective-permute-start(f32[4,4096]{1,0:T(4,128)S(1)} %get-tuple-element.54), channel_id=1, source_target_pairs={{0,64},{64,128},{128,192},{192,0},{1,65},{65,129},{129,193},{193,1... | collective-permute-start | bytes 196616 | tf_op jit(solution)/shard_map/ppermute | solution.py:184
  78.8 0.9 all-to-all-done.2
  79.8 0.7 broadcast_in_dim.26
  80.6 10.9 %all-to-all-start.3 = ((bf16[32,32,128]{2,1,0:T(8,128)(2,1)}), bf16[32,32,128]{2,1,0:T(8,128)(2,1)S(1)}, u32[]{:S(2)}, u32[]{:S(2)}) async-start(bf16[32,32,128]{2,1,0:T(8,128)(2,1)} %broadcast_in_dim.26), calls=%async_computation.3 | async-start | bytes 524288 | tf_op jit(solution)/shard_map/all_to_all | solution.py:200
  91.6 0.7 copy.27
  92.4 0.2 copy.26
  92.6 0.8 reshape.68
  93.4 0.5 slice_bitcast_fusion.8
  93.9 10.4 %all-to-all-done.3 = bf16[32,32,128]{2,1,0:T(8,128)(2,1)S(1)} async-done(((bf16[32,32,128]{2,1,0:T(8,128)(2,1)}), bf16[32,32,128]{2,1,0:T(8,128)(2,1)S(1)}, u32[]{:S(2)}, u32[]{:S(2)}) %all-to-all-start.3) | async-done | bytes 262176 | tf_op jit(solution)/shard_map/all_to_all | solution.py:200
  104.2 0.8 bitcast_convert_fusion
  (37 shorter events, 1.5 us)
Async XLA Ops:
  1.5 16.7 %collective-permute-start.2 = (bf16[4,4096]{1,0:T(4,128)(2,1)S(1)}, bf16[4,4096]{1,0:T(4,128)(2,1)S(1)}, u32[]{:S(2)}, u32[]{:S(2)}) collective-permute-start(bf16[4,4096]{1,0:T(4,128)(2,1)S(1)} %reshape.59), channel_id=1, source_target_pairs={{0,192},{64,0},{128,64},{192,128},{1,193},{65,1},{129,65},{193,129... | collective-permute-start | bytes 98312 | tf_op jit(solution)/shard_map/ppermute | solution.py:184
  8.5 9.8 %collective-permute-start.1 = (bf16[4,4096]{1,0:T(4,128)(2,1)S(1)}, bf16[4,4096]{1,0:T(4,128)(2,1)S(1)}, u32[]{:S(2)}, u32[]{:S(2)}) collective-permute-start(bf16[4,4096]{1,0:T(4,128)(2,1)S(1)} %reshape.59), channel_id=1, source_target_pairs={{0,128},{64,192},{128,0},{192,64},{1,129},{65,193},{129,1},{193,65... | collective-permute-start | bytes 98312 | tf_op jit(solution)/shard_map/ppermute | solution.py:184
  9.4 8.8 %collective-permute-start = (bf16[4,4096]{1,0:T(4,128)(2,1)S(1)}, bf16[4,4096]{1,0:T(4,128)(2,1)S(1)}, u32[]{:S(2)}, u32[]{:S(2)}) collective-permute-start(bf16[4,4096]{1,0:T(4,128)(2,1)S(1)} %reshape.59), channel_id=1, source_target_pairs={{0,64},{64,128},{128,192},{192,0},{1,65},{65,129},{129,193},{193,1... | collective-permute-start | bytes 98312 | tf_op jit(solution)/shard_map/ppermute | solution.py:184
  13.6 14.8 %all-to-all-start = ((bf16[8,16,1024]{2,1,0:T(8,128)(2,1)}), bf16[8,16,1024]{2,1,0:T(8,128)(2,1)S(1)}, u32[]{:S(2)}, u32[]{:S(2)}) async-start(bf16[8,16,1024]{2,1,0:T(8,128)(2,1)} %broadcast_in_dim.11), calls=%async_computation | async-start | bytes 524288 | tf_op jit(solution)/shard_map/all_to_all | solution.py:200
  18.4 5.6 %collective-permute-start.4 = (bf16[4,4,4096]{2,1,0:T(4,128)(2,1)S(1)}, bf16[4,4,4096]{2,1,0:T(4,128)(2,1)S(1)}, u32[]{:S(2)}, u32[]{:S(2)}) collective-permute-start(bf16[4,4,4096]{2,1,0:T(4,128)(2,1)S(1)} %pad_maximum_fusion.2), channel_id=1, source_target_pairs={{0,32},{16,48},{32,0},{48,16},{1,33},{17,49},{33,1},{49,17},{2,34}... | collective-permute-start | bytes 393224 | tf_op jit(solution)/shard_map/ppermute | solution.py:184
  21.2 6.7 %collective-permute-start.3 = (bf16[4,4,4096]{2,1,0:T(4,128)(2,1)S(1)}, bf16[4,4,4096]{2,1,0:T(4,128)(2,1)S(1)}, u32[]{:S(2)}, u32[]{:S(2)}) collective-permute-start(bf16[4,4,4096]{2,1,0:T(4,128)(2,1)S(1)} %pad_maximum_fusion.2), channel_id=1, source_target_pairs={{0,16},{16,32},{32,48},{48,0},{1,17},{17,33},{33,49},{49,1},{2,18}... | collective-permute-start | bytes 393224 | tf_op jit(solution)/shard_map/ppermute | solution.py:184
  21.5 6.3 %collective-permute-start.5 = (bf16[4,4,4096]{2,1,0:T(4,128)(2,1)S(1)}, bf16[4,4,4096]{2,1,0:T(4,128)(2,1)S(1)}, u32[]{:S(2)}, u32[]{:S(2)}) collective-permute-start(bf16[4,4,4096]{2,1,0:T(4,128)(2,1)S(1)} %pad_maximum_fusion.2), channel_id=1, source_target_pairs={{0,48},{16,0},{32,16},{48,32},{1,49},{17,1},{33,17},{49,33},{2,50}... | collective-permute-start | bytes 393224 | tf_op jit(solution)/shard_map/ppermute | solution.py:184
  29.0 3.3 %collective-permute-start.6 = (bf16[4,4,4,4096]{3,2,1,0:T(4,128)(2,1)S(1)}, bf16[4,4,4,4096]{3,2,1,0:T(4,128)(2,1)S(1)}, u32[]{:S(2)}, u32[]{:S(2)}) collective-permute-start(bf16[4,4,4,4096]{3,2,1,0:T(4,128)(2,1)S(1)} %pad_maximum_fusion.mine_ref), channel_id=1, source_target_pairs={{0,8},{8,0},{1,9},{9,1},{2,10},{10,2},{3,11},{11,3},{4,12},{12,4},... | collective-permute-start | bytes 1572872 | tf_op jit(solution)/shard_map/ppermute | solution.py:196
  32.3 1.2 %copy-start = (bf16[32,128,128]{2,1,0:T(8,128)(2,1)S(1)}, bf16[32,128,128]{2,1,0:T(8,128)(2,1)}, u32[]{:S(2)}) copy-start(bf16[32,128,128]{2,1,0:T(8,128)(2,1)} %param.9) | copy-start | bytes 3145732
  42.1 21.4 %all-to-all-start.1 = ((bf16[32,40,128]{2,1,0:T(8,128)(2,1)}), bf16[32,40,128]{2,1,0:T(8,128)(2,1)S(1)}, u32[]{:S(2)}, u32[]{:S(2)}) async-start(bf16[32,40,128]{2,1,0:T(8,128)(2,1)} %get-tuple-element.29), calls=%async_computation.1 | async-start | bytes 655360 | tf_op jit(solution)/shard_map/all_to_all | solution.py:200
  57.7 1.5 %collective-permute-start.10 = (bf16[4,4,4096]{2,1,0:T(4,128)(2,1)S(1)}, bf16[4,4,4096]{2,1,0:T(4,128)(2,1)S(1)}, u32[]{:S(2)}, u32[]{:S(2)}) collective-permute-start(bf16[4,4,4096]{2,1,0:T(4,128)(2,1)S(1)} %get-tuple-element.48), channel_id=1, source_target_pairs={{0,8},{8,0},{1,9},{9,1},{2,10},{10,2},{3,11},{11,3},{4,12},{12,4},... | collective-permute-start | bytes 393224 | tf_op jit(solution)/shard_map/ppermute | solution.py:196
  58.3 1.3 %collective-permute-start.9 = (bf16[4,4,4096]{2,1,0:T(4,128)(2,1)S(1)}, bf16[4,4,4096]{2,1,0:T(4,128)(2,1)S(1)}, u32[]{:S(2)}, u32[]{:S(2)}) collective-permute-start(bf16[4,4,4096]{2,1,0:T(4,128)(2,1)S(1)} %get-tuple-element.49), channel_id=1, source_target_pairs={{0,8},{8,0},{1,9},{9,1},{2,10},{10,2},{3,11},{11,3},{4,12},{12,4},... | collective-permute-start | bytes 393224 | tf_op jit(solution)/shard_map/ppermute | solution.py:196
  58.4 1.4 %collective-permute-start.8 = (bf16[4,4,4096]{2,1,0:T(4,128)(2,1)S(1)}, bf16[4,4,4096]{2,1,0:T(4,128)(2,1)S(1)}, u32[]{:S(2)}, u32[]{:S(2)}) collective-permute-start(bf16[4,4,4096]{2,1,0:T(4,128)(2,1)S(1)} %get-tuple-element.50), channel_id=1, source_target_pairs={{0,8},{8,0},{1,9},{9,1},{2,10},{10,2},{3,11},{11,3},{4,12},{12,4},... | collective-permute-start | bytes 393224 | tf_op jit(solution)/shard_map/ppermute | solution.py:196
  58.8 1.3 %collective-permute-start.7 = (bf16[4,4,4096]{2,1,0:T(4,128)(2,1)S(1)}, bf16[4,4,4096]{2,1,0:T(4,128)(2,1)S(1)}, u32[]{:S(2)}, u32[]{:S(2)}) collective-permute-start(bf16[4,4,4096]{2,1,0:T(4,128)(2,1)S(1)} %get-tuple-element.51), channel_id=1, source_target_pairs={{0,8},{8,0},{1,9},{9,1},{2,10},{10,2},{3,11},{11,3},{4,12},{12,4},... | collective-permute-start | bytes 393224 | tf_op jit(solution)/shard_map/ppermute | solution.py:196
  63.7 9.4 %collective-permute-start.11 = (bf16[4,4,4096]{2,1,0:T(4,128)(2,1)S(1)}, bf16[4,4,4096]{2,1,0:T(4,128)(2,1)S(1)}, u32[]{:S(2)}, u32[]{:S(2)}) collective-permute-start(bf16[4,4,4096]{2,1,0:T(4,128)(2,1)S(1)} %get-tuple-element.45), channel_id=1, source_target_pairs={{0,16},{16,32},{32,48},{48,0},{1,17},{17,33},{33,49},{49,1},{2,18}... | collective-permute-start | bytes 393224 | tf_op jit(solution)/shard_map/ppermute | solution.py:184
  64.4 8.7 %collective-permute-start.13 = (bf16[4,4,4096]{2,1,0:T(4,128)(2,1)S(1)}, bf16[4,4,4096]{2,1,0:T(4,128)(2,1)S(1)}, u32[]{:S(2)}, u32[]{:S(2)}) collective-permute-start(bf16[4,4,4096]{2,1,0:T(4,128)(2,1)S(1)} %get-tuple-element.46), channel_id=1, source_target_pairs={{0,48},{16,0},{32,16},{48,32},{1,49},{17,1},{33,17},{49,33},{2,50}... | collective-permute-start | bytes 393224 | tf_op jit(solution)/shard_map/ppermute | solution.py:184
  66.4 7.0 %collective-permute-start.12 = (bf16[4,4,4096]{2,1,0:T(4,128)(2,1)S(1)}, bf16[4,4,4096]{2,1,0:T(4,128)(2,1)S(1)}, u32[]{:S(2)}, u32[]{:S(2)}) collective-permute-start(bf16[4,4,4096]{2,1,0:T(4,128)(2,1)S(1)} %get-tuple-element.47), channel_id=1, source_target_pairs={{0,32},{16,48},{32,0},{48,16},{1,33},{17,49},{33,1},{49,17},{2,34}... | collective-permute-start | bytes 393224 | tf_op jit(solution)/shard_map/ppermute | solution.py:184
  67.8 11.9 %all-to-all-start.2 = ((bf16[8,24,1024]{2,1,0:T(8,128)(2,1)}), bf16[8,24,1024]{2,1,0:T(8,128)(2,1)S(1)}, u32[]{:S(2)}, u32[]{:S(2)}) async-start(bf16[8,24,1024]{2,1,0:T(8,128)(2,1)} %pad_maximum_fusion.1), calls=%async_computation.2 | async-start | bytes 786432 | tf_op jit(solution)/shard_map/all_to_all | solution.py:200
  73.6 17.9 %collective-permute-start.15 = (f32[4,4096]{1,0:T(4,128)S(1)}, f32[4,4096]{1,0:T(4,128)S(1)}, u32[]{:S(2)}, u32[]{:S(2)}) collective-permute-start(f32[4,4096]{1,0:T(4,128)S(1)} %get-tuple-element.52), channel_id=1, source_target_pairs={{0,128},{64,192},{128,0},{192,64},{1,129},{65,193},{129,1},{193,65... | collective-permute-start | bytes 196616 | tf_op jit(solution)/shard_map/ppermute | solution.py:184
  76.5 15.0 %collective-permute-start.16 = (f32[4,4096]{1,0:T(4,128)S(1)}, f32[4,4096]{1,0:T(4,128)S(1)}, u32[]{:S(2)}, u32[]{:S(2)}) collective-permute-start(f32[4,4096]{1,0:T(4,128)S(1)} %get-tuple-element.53), channel_id=1, source_target_pairs={{0,192},{64,0},{128,64},{192,128},{1,193},{65,1},{129,65},{193,129... | collective-permute-start | bytes 196616 | tf_op jit(solution)/shard_map/ppermute | solution.py:184
  77.2 14.3 %collective-permute-start.14 = (f32[4,4096]{1,0:T(4,128)S(1)}, f32[4,4096]{1,0:T(4,128)S(1)}, u32[]{:S(2)}, u32[]{:S(2)}) collective-permute-start(f32[4,4096]{1,0:T(4,128)S(1)} %get-tuple-element.54), channel_id=1, source_target_pairs={{0,64},{64,128},{128,192},{192,0},{1,65},{65,129},{129,193},{193,1... | collective-permute-start | bytes 196616 | tf_op jit(solution)/shard_map/ppermute | solution.py:184
  80.6 23.7 %all-to-all-start.3 = ((bf16[32,32,128]{2,1,0:T(8,128)(2,1)}), bf16[32,32,128]{2,1,0:T(8,128)(2,1)S(1)}, u32[]{:S(2)}, u32[]{:S(2)}) async-start(bf16[32,32,128]{2,1,0:T(8,128)(2,1)} %broadcast_in_dim.26), calls=%async_computation.3 | async-start | bytes 524288 | tf_op jit(solution)/shard_map/all_to_all | solution.py:200

commit v4 on v1

--- a/solution.py
+++ b/solution.py
@@ -213,23 +213,25 @@
     moved = [swap(r_oth[k]) for k in range(4)]
     wg, l, _ = lax.optimization_barrier((wg, l, moved))
     wg = jnp.sum(wg.astype(F32), axis=0).reshape(5, TI * C)
-    high = lax.reduce_precision(wg, 8, 7)
-    pair = jnp.concatenate([high, wg - high, jnp.zeros((6, TI * C), F32)], axis=0).astype(BF)
     both = exchange(
         jnp.concatenate(
-            [l.reshape(8, 16, TI * C), jnp.broadcast_to(pair[None], (8, 16, TI * C))], axis=1
+            [
+                l.reshape(8, 16, TI * C),
+                jnp.broadcast_to(jnp.pad(wg.astype(BF), ((0, 3), (0, 0)))[None], (8, 8, TI * C)),
+            ],
+            axis=1,
         ),
         COL,
     )
     both = jnp.sum(both.astype(F32), axis=0)
     left_grad = both[:16].reshape(16, TI, C).transpose(1, 0, 2).reshape(TI, 16 * C)
-    wg = (both[16:21] + both[21:26]).reshape(C + 8, CZ) * (1.0 / (TI * 32))
+    wg = both[16:21].reshape(C + 8, CZ) * (1.0 / (TI * 32))
     bias_grad = wg[C]
     full = spread(wg[:C].astype(BF), ROW, 32)
     full, left_grad, bias_grad = lax.optimization_barrier((full, left_grad, bias_grad))
     weight_grad = full.astype(F32).reshape(CC, CZ)
     r = [(r_own[k] + moved[k].astype(F32)).astype(BF) for k in range(4)]
-    right_sum = reduce4(reduce4(r, "x"), "h")
+    right_sum = reduce4(reduce4(r, "x").astype(BF), "h")
     right_grad = right_sum.reshape(4 * C, TJ).T
     return (
         pair_out.reshape(TI, TJ, CZ),

time: 106 us -> 112 us (1.057)
  starting transfers between devices: 46 us -> 49.9 us
  waiting for transfers between devices: 33.6 us -> 34.8 us
    all_to_all x4, starting transfers between devices: 19.5 us -> 22.3 us  [exchange(): return lax.all_to_all(x, axes, split_axis=0, concat_axis=0, tiled=True)]
    ppermute x12, starting transfers between devices: 21.8 us -> 24.5 us  [shift(): return lax.ppermute(x, axis, [(i, (i + k) % 4) for i in range(4)])]
    all_to_all x4, waiting for transfers between devices: 26.4 us -> 28.9 us  [exchange(): return lax.all_to_all(x, axes, split_axis=0, concat_axis=0, tiled=True)]
    ppermute x12, waiting for transfers between devices: 6 us -> 3.88 us  [shift(): return lax.ppermute(x, axis, [(i, (i + k) % 4) for i in range(4)])]
    ppermute x5, starting transfers between devices: 4.62 us -> 3.15 us  [swap(): return lax.ppermute(x, 'c', [(0, 1), (1, 0)])]
  transfers between devices with their start and end apart: 21 -> 21, of which waited for: 7 -> 8; matrix products, arithmetic and copies ran while one was open for 6% -> 5% of each run, Pallas kernels for 0% -> 0%
where the time goes in v4:
time: 112 us; the launch traced here: 111 us
  starting transfers between devices  49.9 us (45%)
  waiting for transfers between devices  34.8 us (31%)
  Pallas kernels  16.1 us (14%)
  local copies, waits for them, and re-layouts  6.27 us (6%)
  other arithmetic  2.94 us (3%)
    all_to_all x4, waiting for transfers between devices, exchange(): return lax.all_to_all(x, axes, split_axis=0, concat_axis=0, tiled=True)  28.9 us
    ppermute x12, starting transfers between devices, shift(): return lax.ppermute(x, axis, [(i, (i + k) % 4) for i in range(4)])  24.5 us
    all_to_all x4, starting transfers between devices, exchange(): return lax.all_to_all(x, axes, split_axis=0, concat_axis=0, tiled=True)  22.3 us
    pallas_call x1, Pallas kernels, forward_call(): pl.pallas_call(forward_kernel, in_specs=[SCALARS] + [WHOLE] * 6, out_spec...  9.11 us
    pallas_call x1, Pallas kernels, backward_call(): pl.pallas_call(backward_kernel, in_specs=[SCALARS, FAR, FAR, WHOLE, WHOLE...  7 us
    ppermute x12, waiting for transfers between devices, shift(): return lax.ppermute(x, axis, [(i, (i + k) % 4) for i in range(4)])  3.88 us
    ppermute x5, starting transfers between devices, swap(): return lax.ppermute(x, 'c', [(0, 1), (1, 0)])  3.15 us
  transfers between devices with their start and end apart: 21, of which 8 were waited for; matrix products, arithmetic and copies ran while one was open for 5% of the time, Pallas kernels for 0%

profile of v4, /device:TPU:1, one launch (start us, length us, event | category | flops | bytes accessed | tf_op | source)
XLA Modules:
  0.0 111.0 jit_solution(12949055880773000772)
XLA Ops:
  0.6 0.9 copy.21
  1.5 6.9 %collective-permute-start.2 = (bf16[4,4096]{1,0:T(4,128)(2,1)S(1)}, bf16[4,4096]{1,0:T(4,128)(2,1)S(1)}, u32[]{:S(2)}, u32[]{:S(2)}) collective-permute-start(bf16[4,4096]{1,0:T(4,128)(2,1)S(1)} %reshape.64), channel_id=1, source_target_pairs={{0,192},{64,0},{128,64},{192,128},{1,193},{65,1},{129,65},{193,129... | collective-permute-start | bytes 98312 | tf_op jit(solution)/shard_map/ppermute | solution.py:177
  8.5 1.0 collective-permute-start.1
  9.4 2.3 %collective-permute-start = (bf16[4,4096]{1,0:T(4,128)(2,1)S(1)}, bf16[4,4096]{1,0:T(4,128)(2,1)S(1)}, u32[]{:S(2)}, u32[]{:S(2)}) collective-permute-start(bf16[4,4096]{1,0:T(4,128)(2,1)S(1)} %reshape.64), channel_id=1, source_target_pairs={{0,64},{64,128},{128,192},{192,0},{1,65},{65,129},{129,193},{193,1... | collective-permute-start | bytes 98312 | tf_op jit(solution)/shard_map/ppermute | solution.py:177
  11.7 0.1 reshape.65
  11.9 0.2 broadcast_in_dim.8
  12.1 0.7 broadcast_in_dim.9
  12.8 4.6 %all-to-all-start = ((bf16[8,16,1024]{2,1,0:T(8,128)(2,1)}), bf16[8,16,1024]{2,1,0:T(8,128)(2,1)S(1)}, u32[]{:S(2)}, u32[]{:S(2)}) async-start(bf16[8,16,1024]{2,1,0:T(8,128)(2,1)} %broadcast_in_dim.9), calls=%async_computation | async-start | bytes 524288 | tf_op jit(solution)/shard_map/all_to_all | solution.py:193
  17.6 2.8 %collective-permute-start.4 = (bf16[4,4,4096]{2,1,0:T(4,128)(2,1)S(1)}, bf16[4,4,4096]{2,1,0:T(4,128)(2,1)S(1)}, u32[]{:S(2)}, u32[]{:S(2)}) collective-permute-start(bf16[4,4,4096]{2,1,0:T(4,128)(2,1)S(1)} %pad_maximum_fusion.2), channel_id=1, source_target_pairs={{0,32},{16,48},{32,0},{48,16},{1,33},{17,49},{33,1},{49,17},{2,34}... | collective-permute-start | bytes 393224 | tf_op jit(solution)/shard_map/ppermute | solution.py:177
  20.5 0.3 collective-permute-start.3
  20.8 2.4 %collective-permute-start.5 = (bf16[4,4,4096]{2,1,0:T(4,128)(2,1)S(1)}, bf16[4,4,4096]{2,1,0:T(4,128)(2,1)S(1)}, u32[]{:S(2)}, u32[]{:S(2)}) collective-permute-start(bf16[4,4,4096]{2,1,0:T(4,128)(2,1)S(1)} %pad_maximum_fusion.2), channel_id=1, source_target_pairs={{0,48},{16,0},{32,16},{48,32},{1,49},{17,1},{33,17},{49,33},{2,50}... | collective-permute-start | bytes 393224 | tf_op jit(solution)/shard_map/ppermute | solution.py:177
  23.3 3.8 %collective-permute-done.3 = bf16[4,4,4096]{2,1,0:T(4,128)(2,1)S(1)} collective-permute-done((bf16[4,4,4096]{2,1,0:T(4,128)(2,1)S(1)}, bf16[4,4,4096]{2,1,0:T(4,128)(2,1)S(1)}, u32[]{:S(2)}, u32[]{:S(2)}) %collective-permute-start.3) | collective-permute-done | bytes 131104 | tf_op jit(solution)/shard_map/ppermute | solution.py:177
  27.1 0.5 pad_maximum_fusion.mine_ref
  27.6 1.8 %collective-permute-start.6 = (bf16[4,4,4,4096]{3,2,1,0:T(4,128)(2,1)S(1)}, bf16[4,4,4,4096]{3,2,1,0:T(4,128)(2,1)S(1)}, u32[]{:S(2)}, u32[]{:S(2)}) collective-permute-start(bf16[4,4,4,4096]{3,2,1,0:T(4,128)(2,1)S(1)} %pad_maximum_fusion.mine_ref), channel_id=1, source_target_pairs={{0,8},{8,0},{1,9},{9,1},{2,10},{10,2},{3,11},{11,3},{4,12},{12,4},... | collective-permute-start | bytes 1572872 | tf_op jit(solution)/shard_map/ppermute | solution.py:189
  29.5 0.1 copy.25.wt_ref
  29.8 1.2 %collective-permute-done.6.other_ref = bf16[4,4,4,4096]{3,2,1,0:T(4,128)(2,1)S(1)} collective-permute-done((bf16[4,4,4,4096]{3,2,1,0:T(4,128)(2,1)S(1)}, bf16[4,4,4,4096]{3,2,1,0:T(4,128)(2,1)S(1)}, u32[]{:S(2)}, u32[]{:S(2)}) %collective-permute-start.6) | collective-permute-done | bytes 524320 | tf_op jit(solution)/shard_map/ppermute | solution.py:189
  31.0 0.7 copy-done.1
  31.6 9.1 %forward.1 = (bf16[4096,128]{1,0:T(8,128)(2,1)}, bf16[4096,128]{1,0:T(8,128)(2,1)S(1)}, bf16[128,4096]{1,0:T(8,128)(2,1)S(1)}, bf16[32,40,128]{2,1,0:T(8,128)(2,1)}) custom-call(s32[3]{0:T(128)S(1)} %pad_add_fusion.pos_ref, bf16[128,1024]{1,0:T(8,128)(2,1)S(1)} %bitcast.73, bf16[4,4,4,4096]{3,2,1,0:T(4,128)(2,1)S(1)} %pad_maximum_fusion.mine_ref, ...), custom_call_target="tpu_custom_call" | custom-call | flops 6442450944 | bytes 4194304 | tf_op jit(solution)/shard_map/forward/pallas_call | solution.py:128
  40.7 7.0 %backward.1 = (f32[4,4,4,4096]{3,2,1,0:T(4,128)S(1)}, bf16[4,4,4,4096]{3,2,1,0:T(4,128)(2,1)S(1)}, bf16[128,1024]{1,0:T(8,128)(2,1)S(1)}) custom-call(s32[3]{0:T(128)S(1)} %pad_add_fusion.pos_ref, bf16[4096,128]{1,0:T(8,128)(2,1)S(1)} %get-tuple-element.23.dp_in, bf16[128,4096]{1,0:T(8,128)(2,1)S(1)} %get-tuple-element.24.b_in, ...), custom_call_target="tpu_custom_call" | custom-call | flops 6442450944 | bytes 4194304 | tf_op jit(solution)/shard_map/backward/pallas_call | solution.py:155
  47.7 0.2 slice_bitcast_fusion
  47.9 0.7 collective-permute-start.10
  48.6 0.1 collective-permute-start.9
  48.8 0.4 collective-permute-start.8
  49.1 0.1 collective-permute-start.7
  49.3 0.3 collective-permute-done.10
  49.6 0.4 collective-permute-done.9
  50.0 0.2 collective-permute-done.8
  50.2 0.2 fusion.2
  50.4 0.5 collective-permute-start.11
  50.8 2.5 %collective-permute-start.13 = (bf16[4,4,4096]{2,1,0:T(4,128)(2,1)S(1)}, bf16[4,4,4096]{2,1,0:T(4,128)(2,1)S(1)}, u32[]{:S(2)}, u32[]{:S(2)}) collective-permute-start(bf16[4,4,4096]{2,1,0:T(4,128)(2,1)S(1)} %get-tuple-element.34), channel_id=1, source_target_pairs={{0,48},{16,0},{32,16},{48,32},{1,49},{17,1},{33,17},{49,33},{2,50}... | collective-permute-start | bytes 393224 | tf_op jit(solution)/shard_map/ppermute | solution.py:177
  53.4 1.1 collective-permute-start.12
  54.5 6.6 %all-to-all-start.1 = ((bf16[32,40,128]{2,1,0:T(8,128)(2,1)}), bf16[32,40,128]{2,1,0:T(8,128)(2,1)S(1)}, u32[]{:S(2)}, u32[]{:S(2)}) async-start(bf16[32,40,128]{2,1,0:T(8,128)(2,1)} %get-tuple-element.22), calls=%async_computation.1 | async-start | bytes 655360 | tf_op jit(solution)/shard_map/all_to_all | solution.py:193
  61.1 0.2 add_convert_fusion
  61.3 14.1 %all-to-all-done.1 = bf16[32,40,128]{2,1,0:T(8,128)(2,1)S(1)} async-done(((bf16[32,40,128]{2,1,0:T(8,128)(2,1)}), bf16[32,40,128]{2,1,0:T(8,128)(2,1)S(1)}, u32[]{:S(2)}, u32[]{:S(2)}) %all-to-all-start.1) | async-done | bytes 327712 | tf_op jit(solution)/shard_map/all_to_all | solution.py:193
  75.6 0.8 pad_maximum_fusion.1
  76.4 5.7 %all-to-all-start.2 = ((bf16[8,24,1024]{2,1,0:T(8,128)(2,1)}), bf16[8,24,1024]{2,1,0:T(8,128)(2,1)S(1)}, u32[]{:S(2)}, u32[]{:S(2)}) async-start(bf16[8,24,1024]{2,1,0:T(8,128)(2,1)} %pad_maximum_fusion.1), calls=%async_computation.2 | async-start | bytes 786432 | tf_op jit(solution)/shard_map/all_to_all | solution.py:193
  82.1 0.6 collective-permute-start.14
  82.6 3.1 %collective-permute-start.16 = (bf16[4,4096]{1,0:T(4,128)(2,1)S(1)}, bf16[4,4096]{1,0:T(4,128)(2,1)S(1)}, u32[]{:S(2)}, u32[]{:S(2)}) collective-permute-start(bf16[4,4096]{1,0:T(4,128)(2,1)S(1)} %get-tuple-element.41), channel_id=1, source_target_pairs={{0,192},{64,0},{128,64},{192,128},{1,193},{65,1},{129,65},{193,129... | collective-permute-start | bytes 98312 | tf_op jit(solution)/shard_map/ppermute | solution.py:177
  85.7 1.1 collective-permute-start.15
  86.8 3.2 %all-to-all-done.2 = bf16[8,24,1024]{2,1,0:T(8,128)(2,1)S(1)} async-done(((bf16[8,24,1024]{2,1,0:T(8,128)(2,1)}), bf16[8,24,1024]{2,1,0:T(8,128)(2,1)S(1)}, u32[]{:S(2)}, u32[]{:S(2)}) %all-to-all-start.2) | async-done | bytes 393248 | tf_op jit(solution)/shard_map/all_to_all | solution.py:193
  90.2 0.7 broadcast_in_dim.22
  90.9 5.4 %all-to-all-start.3 = ((bf16[32,32,128]{2,1,0:T(8,128)(2,1)}), bf16[32,32,128]{2,1,0:T(8,128)(2,1)S(1)}, u32[]{:S(2)}, u32[]{:S(2)}) async-start(bf16[32,32,128]{2,1,0:T(8,128)(2,1)} %broadcast_in_dim.22), calls=%async_computation.3 | async-start | bytes 524288 | tf_op jit(solution)/shard_map/all_to_all | solution.py:193
  96.4 0.7 copy.27
  97.2 0.2 copy.26
  97.4 0.8 reshape.74
  98.2 0.5 slice_bitcast_fusion.8
  98.7 11.5 %all-to-all-done.3 = bf16[32,32,128]{2,1,0:T(8,128)(2,1)S(1)} async-done(((bf16[32,32,128]{2,1,0:T(8,128)(2,1)}), bf16[32,32,128]{2,1,0:T(8,128)(2,1)S(1)}, u32[]{:S(2)}, u32[]{:S(2)}) %all-to-all-start.3) | async-done | bytes 262176 | tf_op jit(solution)/shard_map/all_to_all | solution.py:193
  110.2 0.8 bitcast_convert_fusion
  (42 shorter events, 1.0 us)
Async XLA Ops:
  1.5 10.2 %copy-start.3 = (bf16[32,512]{1,0:T(8,128)(2,1)S(1)}, bf16[32,512]{1,0:T(8,128)(2,1)}, u32[]{:S(2)}) copy-start(bf16[32,512]{1,0:T(8,128)(2,1)} %param.5) | copy-start | bytes 98308
  1.5 15.9 %collective-permute-start.2 = (bf16[4,4096]{1,0:T(4,128)(2,1)S(1)}, bf16[4,4096]{1,0:T(4,128)(2,1)S(1)}, u32[]{:S(2)}, u32[]{:S(2)}) collective-permute-start(bf16[4,4096]{1,0:T(4,128)(2,1)S(1)} %reshape.64), channel_id=1, source_target_pairs={{0,192},{64,0},{128,64},{192,128},{1,193},{65,1},{129,65},{193,129... | collective-permute-start | bytes 98312 | tf_op jit(solution)/shard_map/ppermute | solution.py:177
  8.5 9.0 %collective-permute-start.1 = (bf16[4,4096]{1,0:T(4,128)(2,1)S(1)}, bf16[4,4096]{1,0:T(4,128)(2,1)S(1)}, u32[]{:S(2)}, u32[]{:S(2)}) collective-permute-start(bf16[4,4096]{1,0:T(4,128)(2,1)S(1)} %reshape.64), channel_id=1, source_target_pairs={{0,128},{64,192},{128,0},{192,64},{1,129},{65,193},{129,1},{193,65... | collective-permute-start | bytes 98312 | tf_op jit(solution)/shard_map/ppermute | solution.py:177
  9.4 8.0 %collective-permute-start = (bf16[4,4096]{1,0:T(4,128)(2,1)S(1)}, bf16[4,4096]{1,0:T(4,128)(2,1)S(1)}, u32[]{:S(2)}, u32[]{:S(2)}) collective-permute-start(bf16[4,4096]{1,0:T(4,128)(2,1)S(1)} %reshape.64), channel_id=1, source_target_pairs={{0,64},{64,128},{128,192},{192,0},{1,65},{65,129},{129,193},{193,1... | collective-permute-start | bytes 98312 | tf_op jit(solution)/shard_map/ppermute | solution.py:177
  12.8 14.8 %all-to-all-start = ((bf16[8,16,1024]{2,1,0:T(8,128)(2,1)}), bf16[8,16,1024]{2,1,0:T(8,128)(2,1)S(1)}, u32[]{:S(2)}, u32[]{:S(2)}) async-start(bf16[8,16,1024]{2,1,0:T(8,128)(2,1)} %broadcast_in_dim.9), calls=%async_computation | async-start | bytes 524288 | tf_op jit(solution)/shard_map/all_to_all | solution.py:193
  17.6 5.6 %collective-permute-start.4 = (bf16[4,4,4096]{2,1,0:T(4,128)(2,1)S(1)}, bf16[4,4,4096]{2,1,0:T(4,128)(2,1)S(1)}, u32[]{:S(2)}, u32[]{:S(2)}) collective-permute-start(bf16[4,4,4096]{2,1,0:T(4,128)(2,1)S(1)} %pad_maximum_fusion.2), channel_id=1, source_target_pairs={{0,32},{16,48},{32,0},{48,16},{1,33},{17,49},{33,1},{49,17},{2,34}... | collective-permute-start | bytes 393224 | tf_op jit(solution)/shard_map/ppermute | solution.py:177
  20.5 6.7 %collective-permute-start.3 = (bf16[4,4,4096]{2,1,0:T(4,128)(2,1)S(1)}, bf16[4,4,4096]{2,1,0:T(4,128)(2,1)S(1)}, u32[]{:S(2)}, u32[]{:S(2)}) collective-permute-start(bf16[4,4,4096]{2,1,0:T(4,128)(2,1)S(1)} %pad_maximum_fusion.2), channel_id=1, source_target_pairs={{0,16},{16,32},{32,48},{48,0},{1,17},{17,33},{33,49},{49,1},{2,18}... | collective-permute-start | bytes 393224 | tf_op jit(solution)/shard_map/ppermute | solution.py:177
  20.8 6.3 %collective-permute-start.5 = (bf16[4,4,4096]{2,1,0:T(4,128)(2,1)S(1)}, bf16[4,4,4096]{2,1,0:T(4,128)(2,1)S(1)}, u32[]{:S(2)}, u32[]{:S(2)}) collective-permute-start(bf16[4,4,4096]{2,1,0:T(4,128)(2,1)S(1)} %pad_maximum_fusion.2), channel_id=1, source_target_pairs={{0,48},{16,0},{32,16},{48,32},{1,49},{17,1},{33,17},{49,33},{2,50}... | collective-permute-start | bytes 393224 | tf_op jit(solution)/shard_map/ppermute | solution.py:177
  23.1 6.3 %copy-start.2 = (bf16[1024,128]{1,0:T(8,128)(2,1)S(1)}, bf16[1024,128]{1,0:T(8,128)(2,1)}, u32[]{:S(2)}) copy-start(bf16[1024,128]{1,0:T(8,128)(2,1)} %param.7) | copy-start | bytes 786436
  27.1 3.8 %copy-start = (bf16[32,128,128]{2,1,0:T(8,128)(2,1)S(1)}, bf16[32,128,128]{2,1,0:T(8,128)(2,1)}, u32[]{:S(2)}) copy-start(bf16[32,128,128]{2,1,0:T(8,128)(2,1)} %param.9) | copy-start | bytes 3145732
  27.6 3.4 %collective-permute-start.6 = (bf16[4,4,4,4096]{3,2,1,0:T(4,128)(2,1)S(1)}, bf16[4,4,4,4096]{3,2,1,0:T(4,128)(2,1)S(1)}, u32[]{:S(2)}, u32[]{:S(2)}) collective-permute-start(bf16[4,4,4,4096]{3,2,1,0:T(4,128)(2,1)S(1)} %pad_maximum_fusion.mine_ref), channel_id=1, source_target_pairs={{0,8},{8,0},{1,9},{9,1},{2,10},{10,2},{3,11},{11,3},{4,12},{12,4},... | collective-permute-start | bytes 1572872 | tf_op jit(solution)/shard_map/ppermute | solution.py:189
  31.0 0.7 copy-start.1
  47.9 1.7 %collective-permute-start.10 = (bf16[4,4,4096]{2,1,0:T(4,128)(2,1)S(1)}, bf16[4,4,4096]{2,1,0:T(4,128)(2,1)S(1)}, u32[]{:S(2)}, u32[]{:S(2)}) collective-permute-start(bf16[4,4,4096]{2,1,0:T(4,128)(2,1)S(1)} %get-tuple-element.36), channel_id=1, source_target_pairs={{0,8},{8,0},{1,9},{9,1},{2,10},{10,2},{3,11},{11,3},{4,12},{12,4},... | collective-permute-start | bytes 393224 | tf_op jit(solution)/shard_map/ppermute | solution.py:189
  48.6 1.3 %collective-permute-start.9 = (bf16[4,4,4096]{2,1,0:T(4,128)(2,1)S(1)}, bf16[4,4,4096]{2,1,0:T(4,128)(2,1)S(1)}, u32[]{:S(2)}, u32[]{:S(2)}) collective-permute-start(bf16[4,4,4096]{2,1,0:T(4,128)(2,1)S(1)} %get-tuple-element.37), channel_id=1, source_target_pairs={{0,8},{8,0},{1,9},{9,1},{2,10},{10,2},{3,11},{11,3},{4,12},{12,4},... | collective-permute-start | bytes 393224 | tf_op jit(solution)/shard_map/ppermute | solution.py:189
  48.8 1.4 %collective-permute-start.8 = (bf16[4,4,4096]{2,1,0:T(4,128)(2,1)S(1)}, bf16[4,4,4096]{2,1,0:T(4,128)(2,1)S(1)}, u32[]{:S(2)}, u32[]{:S(2)}) collective-permute-start(bf16[4,4,4096]{2,1,0:T(4,128)(2,1)S(1)} %get-tuple-element.38), channel_id=1, source_target_pairs={{0,8},{8,0},{1,9},{9,1},{2,10},{10,2},{3,11},{11,3},{4,12},{12,4},... | collective-permute-start | bytes 393224 | tf_op jit(solution)/shard_map/ppermute | solution.py:189
  49.1 12.0 %collective-permute-start.7 = (bf16[4,4,4096]{2,1,0:T(4,128)(2,1)S(1)}, bf16[4,4,4096]{2,1,0:T(4,128)(2,1)S(1)}, u32[]{:S(2)}, u32[]{:S(2)}) collective-permute-start(bf16[4,4,4096]{2,1,0:T(4,128)(2,1)S(1)} %get-tuple-element.39), channel_id=1, source_target_pairs={{0,8},{8,0},{1,9},{9,1},{2,10},{10,2},{3,11},{11,3},{4,12},{12,4},... | collective-permute-start | bytes 393224 | tf_op jit(solution)/shard_map/ppermute | solution.py:189
  50.4 10.7 %collective-permute-start.11 = (bf16[4,4,4096]{2,1,0:T(4,128)(2,1)S(1)}, bf16[4,4,4096]{2,1,0:T(4,128)(2,1)S(1)}, u32[]{:S(2)}, u32[]{:S(2)}) collective-permute-start(bf16[4,4,4096]{2,1,0:T(4,128)(2,1)S(1)} %get-tuple-element.33), channel_id=1, source_target_pairs={{0,16},{16,32},{32,48},{48,0},{1,17},{17,33},{33,49},{49,1},{2,18}... | collective-permute-start | bytes 393224 | tf_op jit(solution)/shard_map/ppermute | solution.py:177
  50.8 10.3 %collective-permute-start.13 = (bf16[4,4,4096]{2,1,0:T(4,128)(2,1)S(1)}, bf16[4,4,4096]{2,1,0:T(4,128)(2,1)S(1)}, u32[]{:S(2)}, u32[]{:S(2)}) collective-permute-start(bf16[4,4,4096]{2,1,0:T(4,128)(2,1)S(1)} %get-tuple-element.34), channel_id=1, source_target_pairs={{0,48},{16,0},{32,16},{48,32},{1,49},{17,1},{33,17},{49,33},{2,50}... | collective-permute-start | bytes 393224 | tf_op jit(solution)/shard_map/ppermute | solution.py:177
  53.4 7.8 %collective-permute-start.12 = (bf16[4,4,4096]{2,1,0:T(4,128)(2,1)S(1)}, bf16[4,4,4096]{2,1,0:T(4,128)(2,1)S(1)}, u32[]{:S(2)}, u32[]{:S(2)}) collective-permute-start(bf16[4,4,4096]{2,1,0:T(4,128)(2,1)S(1)} %get-tuple-element.35), channel_id=1, source_target_pairs={{0,32},{16,48},{32,0},{48,16},{1,33},{17,49},{33,1},{49,17},{2,34}... | collective-permute-start | bytes 393224 | tf_op jit(solution)/shard_map/ppermute | solution.py:177
  54.5 21.0 %all-to-all-start.1 = ((bf16[32,40,128]{2,1,0:T(8,128)(2,1)}), bf16[32,40,128]{2,1,0:T(8,128)(2,1)S(1)}, u32[]{:S(2)}, u32[]{:S(2)}) async-start(bf16[32,40,128]{2,1,0:T(8,128)(2,1)} %get-tuple-element.22), calls=%async_computation.1 | async-start | bytes 655360 | tf_op jit(solution)/shard_map/all_to_all | solution.py:193
  76.4 13.7 %all-to-all-start.2 = ((bf16[8,24,1024]{2,1,0:T(8,128)(2,1)}), bf16[8,24,1024]{2,1,0:T(8,128)(2,1)S(1)}, u32[]{:S(2)}, u32[]{:S(2)}) async-start(bf16[8,24,1024]{2,1,0:T(8,128)(2,1)} %pad_maximum_fusion.1), calls=%async_computation.2 | async-start | bytes 786432 | tf_op jit(solution)/shard_map/all_to_all | solution.py:193
  82.1 14.2 %collective-permute-start.14 = (bf16[4,4096]{1,0:T(4,128)(2,1)S(1)}, bf16[4,4096]{1,0:T(4,128)(2,1)S(1)}, u32[]{:S(2)}, u32[]{:S(2)}) collective-permute-start(bf16[4,4096]{1,0:T(4,128)(2,1)S(1)} %get-tuple-element.40), channel_id=1, source_target_pairs={{0,64},{64,128},{128,192},{192,0},{1,65},{65,129},{129,193},{193,1... | collective-permute-start | bytes 98312 | tf_op jit(solution)/shard_map/ppermute | solution.py:177
  82.6 13.6 %collective-permute-start.16 = (bf16[4,4096]{1,0:T(4,128)(2,1)S(1)}, bf16[4,4096]{1,0:T(4,128)(2,1)S(1)}, u32[]{:S(2)}, u32[]{:S(2)}) collective-permute-start(bf16[4,4096]{1,0:T(4,128)(2,1)S(1)} %get-tuple-element.41), channel_id=1, source_target_pairs={{0,192},{64,0},{128,64},{192,128},{1,193},{65,1},{129,65},{193,129... | collective-permute-start | bytes 98312 | tf_op jit(solution)/shard_map/ppermute | solution.py:177
  85.7 10.6 %collective-permute-start.15 = (bf16[4,4096]{1,0:T(4,128)(2,1)S(1)}, bf16[4,4096]{1,0:T(4,128)(2,1)S(1)}, u32[]{:S(2)}, u32[]{:S(2)}) collective-permute-start(bf16[4,4096]{1,0:T(4,128)(2,1)S(1)} %get-tuple-element.42), channel_id=1, source_target_pairs={{0,128},{64,192},{128,0},{192,64},{1,129},{65,193},{129,1},{193,65... | collective-permute-start | bytes 98312 | tf_op jit(solution)/shard_map/ppermute | solution.py:177
  90.9 19.3 %all-to-all-start.3 = ((bf16[32,32,128]{2,1,0:T(8,128)(2,1)}), bf16[32,32,128]{2,1,0:T(8,128)(2,1)S(1)}, u32[]{:S(2)}, u32[]{:S(2)}) async-start(bf16[32,32,128]{2,1,0:T(8,128)(2,1)} %broadcast_in_dim.22), calls=%async_computation.3 | async-start | bytes 524288 | tf_op jit(solution)/shard_map/all_to_all | solution.py:193
